TPU v7x, 128 devices: a whole 4x4x4 slice. The times are simulated.
128 devices in a mesh: dp: 16 (over x, z), seq: 8 (over y, core).
Axes of the slice: x: 4, y: 4, z: 4, core: 2. Of those that a mesh axis runs over, the one named last changes fastest.
Arguments:
- query_rows: bfloat16 [16384, 4096], P(('dp', 'seq')), may hold values from -60 to 60
- key_rows: bfloat16 [16384, 4096], P(('dp', 'seq')), may hold values from -5 to 5
- value_rows: bfloat16 [16384, 4096], P(('dp', 'seq')), may hold values from -12 to 12
- seg_ids: int32 [16384], P(('dp', 'seq')), may hold values from 0 to 31, as said below
- timesteps: int32 [32], replicated, may hold values from 0 to 999
- w_mod: bfloat16 [256, 4096], replicated, may hold values from -0.375 to 0.375
Outputs:
- mixed_rows: bfloat16 [16384, 4096], P(('dp', 'seq'))
Inputs may be any that keep to these rules, and one draw needn't show every extreme that they name: A row's bin is seg_ids // 2, a number below the size of dp. The 128 rows of one device hold at most 16 rows of any one bin, and for every index of seq some bin holds exactly 16 rows on each device of that index. Rows of one sample lie on many devices.
All inputs are finite; a program needn't handle non-finite values.
Results may differ from a plain program's by a relative error of at most 0.0058.
Values may be sent and summed in bfloat16 or wider, within the bound.
No kernel may reach another device: no remote copies, remote signals or barrier semaphores. Data moves between devices by JAX's collectives and lax.ppermute only.
A program may use at most 128 MiB of HBM per device.

v0:
```python
import math

import jax
import jax.numpy as jnp
from jax import lax
from jax.sharding import PartitionSpec as P

HEAD_DIM = 128
FREQ = 256
SEG_BIN = 2


def for_sending(value):
    return jax.tree.map(lambda a: a.astype(jnp.bfloat16) if a.dtype == jnp.float32 else a, value)


def scale_rows_table(timesteps, w_mod):
    half_freq = FREQ // 2
    frequencies = jnp.exp(-math.log(10000.0) * jnp.arange(half_freq, dtype=jnp.float32) / half_freq)
    angles = timesteps.astype(jnp.float32)[:, None] * frequencies[None, :]
    embedding = jnp.concatenate([jnp.cos(angles), jnp.sin(angles)], axis=1)
    activated = jax.nn.silu(embedding).astype(jnp.bfloat16)
    return jnp.dot(activated, w_mod, preferred_element_type=jnp.float32)


def slot_places(row_bins, bin_count, capacity):
    bin_hits = (row_bins[:, None] == jnp.arange(bin_count, dtype=jnp.int32)[None, :]).astype(
        jnp.int32
    )
    ranks = jnp.cumsum(bin_hits, axis=0) - bin_hits
    slot_rank = jnp.sum(ranks * bin_hits, axis=1)
    target = row_bins * capacity + slot_rank
    return jnp.arange(bin_count * capacity, dtype=jnp.int32)[:, None] == target[None, :]


def slot_ids_of(placement, sample_ids):
    return jnp.sum(jnp.where(placement, sample_ids[None, :] + 1, 0), axis=1) - 1


def attend_slots(query_part, key_part, value_part, sample_ids):
    length, row_width = query_part.shape
    head_count = row_width // HEAD_DIM
    block_rows = min(512, length)
    score_scale = 1.0 / math.sqrt(HEAD_DIM)
    query_blocks = query_part.reshape(length // block_rows, block_rows, head_count, HEAD_DIM)
    key_heads = key_part.reshape(length, head_count, HEAD_DIM)
    value_heads = value_part.reshape(length, head_count, HEAD_DIM)
    id_blocks = sample_ids.reshape(length // block_rows, block_rows)

    def one_block(block_pair):
        query_block, query_ids = block_pair
        scores = (
            jnp.einsum("qhd,khd->hqk", query_block, key_heads, preferred_element_type=jnp.float32)
            * score_scale
        )
        same_sample = query_ids[:, None] == sample_ids[None, :]
        scores = jnp.where(same_sample[None], scores, -1e30)
        row_max = jnp.max(scores, axis=2, keepdims=True)
        weights = jnp.exp(scores - row_max)
        soft_probs = (weights / jnp.sum(weights, axis=2, keepdims=True)).astype(jnp.bfloat16)
        block_out = jnp.einsum(
            "hqk,khd->qhd", soft_probs, value_heads, preferred_element_type=jnp.float32
        )
        return block_out.astype(jnp.bfloat16).reshape(block_rows, row_width)

    return lax.map(one_block, (query_blocks, id_blocks)).reshape(length, row_width)


def place_rows(place_mask, arrays):
    return tuple(
        (
            jnp.dot(place_mask, single, preferred_element_type=jnp.float32).astype(jnp.bfloat16)
            for single in arrays
        )
    )


def shards(query_rows, key_rows, value_rows, seg_ids, timesteps, w_mod):
    dp_count = lax.axis_size("dp")
    seq_count = lax.axis_size("seq")
    row_count = query_rows.shape[0]
    capacity = 2 * row_count // dp_count
    ids_tiled = jnp.broadcast_to(seg_ids[:, None], (row_count, seq_count))
    group_ids = lax.all_to_all(ids_tiled, "seq", split_axis=1, concat_axis=0, tiled=True).reshape(
        -1
    )
    head_parts = (
        lax.all_to_all(query_rows, "seq", split_axis=1, concat_axis=0, tiled=True),
        lax.all_to_all(key_rows, "seq", split_axis=1, concat_axis=0, tiled=True),
        lax.all_to_all(value_rows, "seq", split_axis=1, concat_axis=0, tiled=True),
    )
    placement = slot_places(group_ids // SEG_BIN, dp_count, seq_count * capacity)
    place_mask = placement.astype(jnp.bfloat16)
    slotted = place_rows(place_mask, head_parts)
    bin_ids = lax.all_to_all(
        slot_ids_of(placement, group_ids), "dp", split_axis=0, concat_axis=0, tiled=True
    )
    bin_query, bin_key, bin_value = jax.tree.map(
        lambda part, own: part.astype(own.dtype),
        lax.all_to_all(for_sending(slotted), "dp", split_axis=0, concat_axis=0, tiled=True),
        slotted,
    )
    attended = attend_slots(bin_query, bin_key, bin_value, bin_ids)
    returned = lax.all_to_all(attended, "dp", split_axis=0, concat_axis=0, tiled=True)
    unslotted = jnp.dot(place_mask.T, returned, preferred_element_type=jnp.float32).astype(
        jnp.bfloat16
    )
    home_rows = lax.all_to_all(unslotted, "seq", split_axis=0, concat_axis=1, tiled=True)
    scale_table = scale_rows_table(timesteps, w_mod)
    lookup = (
        seg_ids[:, None] == jnp.arange(scale_table.shape[0], dtype=jnp.int32)[None, :]
    ).astype(jnp.float32)
    row_scales = jnp.dot(
        lookup, scale_table, precision=lax.Precision.HIGHEST, preferred_element_type=jnp.float32
    )
    return (home_rows.astype(jnp.float32) * (1.0 + row_scales)).astype(jnp.bfloat16)


def solution(mesh):
    placed = (
        P(("dp", "seq"), None),
        P(("dp", "seq"), None),
        P(("dp", "seq"), None),
        P(("dp", "seq")),
        P(),
        P(),
    )
    return jax.shard_map(
        shards, mesh=mesh, in_specs=placed, out_specs=P(("dp", "seq"), None), check_vma=False
    )
```

profile of v0, /device:TPU:1, one launch (start us, length us, event | category | flops | bytes accessed | tf_op | source)
XLA Modules:
  0.0 350.5 jit_solution(14382922364887955043)
XLA Ops:
  1.4 6.0 %all-to-all-start = ((s32[128,8,1]{0,2,1:T(1,128)}), s32[128,8,1]{0,2,1:T(1,128)S(1)}, u32[]{:S(2)}, u32[]{:S(2)}) async-start(s32[128,8,1]{0,2,1:T(1,128)} %broadcast_in_dim.37), calls=%async_computation | async-start | bytes 8192 | tf_op jit(solution)/shard_map/all_to_all | solution.py:84
  7.4 4.5 %all-to-all-done = s32[128,8,1]{0,2,1:T(1,128)S(1)} async-done(((s32[128,8,1]{0,2,1:T(1,128)}), s32[128,8,1]{0,2,1:T(1,128)S(1)}, u32[]{:S(2)}, u32[]{:S(2)}) %all-to-all-start) | async-done | bytes 4128 | tf_op jit(solution)/shard_map/all_to_all | solution.py:84
  11.9 4.5 %reduce-window.6 = s32[16,8,128]{2,1,0:T(8,128)S(1)} reduce-window(s32[16,8,128]{2,1,0:T(8,128)S(1)} %fusion.29, s32[]{:T(128)} %copy.93), window={size=1x1x128 pad=0_0x0_0x127_0}, to_apply=%region_0.1 | reduce-window | flops 2080768 | bytes 131076 | tf_op jit(solution)/shard_map/reduce-window
  18.4 7.6 %all-to-all-start.1 = ((s32[16,128,1]{1,2,0:T(1,128)}), s32[16,128,1]{1,2,0:T(1,128)S(1)}, u32[]{:S(2)}, u32[]{:S(2)}) async-start(s32[16,128,1]{1,2,0:T(1,128)} %bitcast.11), calls=%async_computation.1 | async-start | bytes 16384 | tf_op jit(solution)/shard_map/all_to_all | solution.py:95
  32.4 5.6 %all-to-all-start.4 = ((bf16[128,8,512]{0,2,1:T(8,128)(2,1)}), bf16[128,8,512]{0,2,1:T(8,128)(2,1)S(1)}, u32[]{:S(2)}, u32[]{:S(2)}) async-start(bf16[128,8,512]{0,2,1:T(8,128)(2,1)} %bitcast.88), calls=%async_computation.4 | async-start | bytes 2097152 | tf_op jit(solution)/shard_map/all_to_all | solution.py:89
  40.3 12.8 %all-to-all-done.4 = bf16[128,8,512]{0,2,1:T(8,128)(2,1)S(1)} async-done(((bf16[128,8,512]{0,2,1:T(8,128)(2,1)}), bf16[128,8,512]{0,2,1:T(8,128)(2,1)S(1)}, u32[]{:S(2)}, u32[]{:S(2)}) %all-to-all-start.4) | async-done | bytes 1048608 | tf_op jit(solution)/shard_map/all_to_all | solution.py:89
  54.1 4.3 %all-to-all-start.6 = ((bf16[128,8,512]{0,2,1:T(8,128)(2,1)}), bf16[128,8,512]{0,2,1:T(8,128)(2,1)S(1)}, u32[]{:S(2)}, u32[]{:S(2)}) async-start(bf16[128,8,512]{0,2,1:T(8,128)(2,1)} %bitcast.89), calls=%async_computation.6 | async-start | bytes 2097152 | tf_op jit(solution)/shard_map/all_to_all | solution.py:90
  60.7 12.9 %all-to-all-done.6 = bf16[128,8,512]{0,2,1:T(8,128)(2,1)S(1)} async-done(((bf16[128,8,512]{0,2,1:T(8,128)(2,1)}), bf16[128,8,512]{0,2,1:T(8,128)(2,1)S(1)}, u32[]{:S(2)}, u32[]{:S(2)}) %all-to-all-start.6) | async-done | bytes 1048608 | tf_op jit(solution)/shard_map/all_to_all | solution.py:90
  74.5 4.3 %all-to-all-start.2 = ((bf16[128,8,512]{0,2,1:T(8,128)(2,1)}), bf16[128,8,512]{0,2,1:T(8,128)(2,1)S(1)}, u32[]{:S(2)}, u32[]{:S(2)}) async-start(bf16[128,8,512]{0,2,1:T(8,128)(2,1)} %bitcast.87), calls=%async_computation.2 | async-start | bytes 2097152 | tf_op jit(solution)/shard_map/all_to_all | solution.py:88
  81.1 4.9 %fusion.23 = bf16[2048,512]{1,0:T(8,128)(2,1)} fusion(bf16[1024,512]{1,0:T(8,128)(2,1)} %bitcast.96, s32[1024]{0:T(1024)S(1)} %get-tuple-element.87), kind=kOutput, calls=%fused_computation.33 | convolution fusion | flops 2150629376 | bytes 3149824 | tf_op jit(solution)/shard_map/dot_general | solution.py:72
  94.0 4.4 %all-to-all-start.5 = ((bf16[16,128,512]{1,2,0:T(8,128)(2,1)}), bf16[16,128,512]{1,2,0:T(8,128)(2,1)}, u32[]{:S(2)}, u32[]{:S(2)}) async-start(bf16[16,128,512]{1,2,0:T(8,128)(2,1)} %copy.54), calls=%async_computation.5 | async-start | bytes 4194304 | tf_op jit(solution)/shard_map/all_to_all | solution.py:100
  100.7 4.9 %fusion.24 = bf16[2048,512]{1,0:T(8,128)(2,1)} fusion(bf16[1024,512]{1,0:T(8,128)(2,1)} %bitcast.97, s32[1024]{0:T(1024)S(1)} %get-tuple-element.87), kind=kOutput, calls=%fused_computation.34 | convolution fusion | flops 2150629376 | bytes 3149824 | tf_op jit(solution)/shard_map/dot_general | solution.py:72
  105.6 21.1 %all-to-all-done.5 = bf16[16,128,512]{1,2,0:T(8,128)(2,1)} async-done(((bf16[16,128,512]{1,2,0:T(8,128)(2,1)}), bf16[16,128,512]{1,2,0:T(8,128)(2,1)}, u32[]{:S(2)}, u32[]{:S(2)}) %all-to-all-start.5) | async-done | bytes 2097184 | tf_op jit(solution)/shard_map/all_to_all | solution.py:100
  126.7 4.4 %all-to-all-start.7 = ((bf16[16,128,512]{2,1,0:T(8,128)(2,1)}), bf16[16,128,512]{2,1,0:T(8,128)(2,1)}, u32[]{:S(2)}, u32[]{:S(2)}) async-start(bf16[16,128,512]{2,1,0:T(8,128)(2,1)} %bitcast.92), calls=%async_computation.7 | async-start | bytes 4194304 | tf_op jit(solution)/shard_map/all_to_all | solution.py:100
  132.5 4.9 %fusion.22 = bf16[2048,512]{1,0:T(8,128)(2,1)} fusion(bf16[1024,512]{1,0:T(8,128)(2,1)} %bitcast.98, s32[1024]{0:T(1024)S(1)} %get-tuple-element.87), kind=kOutput, calls=%fused_computation.32 | convolution fusion | flops 2150629376 | bytes 3149824 | tf_op jit(solution)/shard_map/dot_general | solution.py:72
  137.4 19.1 %all-to-all-done.7 = bf16[16,128,512]{2,1,0:T(8,128)(2,1)} async-done(((bf16[16,128,512]{2,1,0:T(8,128)(2,1)}), bf16[16,128,512]{2,1,0:T(8,128)(2,1)}, u32[]{:S(2)}, u32[]{:S(2)}) %all-to-all-start.7) | async-done | bytes 2097184 | tf_op jit(solution)/shard_map/all_to_all | solution.py:100
  156.5 6.6 %all-to-all-start.3 = ((bf16[16,128,512]{2,1,0:T(8,128)(2,1)}), bf16[16,128,512]{2,1,0:T(8,128)(2,1)}, u32[]{:S(2)}, u32[]{:S(2)}) async-start(bf16[16,128,512]{2,1,0:T(8,128)(2,1)} %bitcast.91), calls=%async_computation.3 | async-start | bytes 4194304 | tf_op jit(solution)/shard_map/all_to_all | solution.py:100
  164.3 4.3 %copy.55 = bf16[16,128,512]{1,0,2:T(8,128)(2,1)} copy(bf16[16,128,512]{1,2,0:T(8,128)(2,1)} %all-to-all-done.5) | data formatting | bytes 4194304 | tf_op jit(solution)/shard_map/all_to_all | solution.py:100
  168.5 4.1 %reshape.201 = bf16[2048,4,128]{0,2,1:T(8,128)(2,1)} reshape(bf16[16,128,512]{1,0,2:T(8,128)(2,1)} %copy.55) | data formatting | bytes 4194304 | tf_op jit(solution)/shard_map/reshape | solution.py:46
  180.6 4.3 %copy.63 = bf16[2048,4,128]{0,2,1:T(8,128)(2,1)} copy(bf16[2048,4,128]{2,1,0:T(4,128)(2,1)} %reshape.204) | data formatting | bytes 4194304 | tf_op jit(solution)/shard_map/reshape | solution.py:47
  192.1 96.5 %while.10 = (s32[]{:T(128)}, bf16[4,512,512]{2,1,0:T(8,128)(2,1)}, s32[4,512]{1,0:T(4,128)S(1)}, s32[2048]{0:T(1024)S(1)}, bf16[4,512,4,128]{3,2,1,0:T(4,128)(2,...) while((s32[]{:T(128)}, bf16[4,512,512]{2,1,0:T(8,128)(2,1)}, ...), condition=%wide.region_7.8_spmd, body=%wide.region_4.7_spmd.sunk | while | flops 2173962240 | bytes 44071516 | solution.py:66
  194.8 11.0 %fusion.55 = (f32[4,512]{1,0:T(4,128)S(1)}, f32[4,512,2048]{2,1,0:T(8,128)}) fusion(pred[512,2048]{1,0:T(8,128)(4,1)S(1)} %broadcast_compare_fusion.2, bf16[2048,4,128]{2,0,1:T(8,128)(2,1)} %get-tuple-element.159, bf16[1,512,4,128]{3,2,1,0:T(4,128)(2,1)} %constant_dynamic-slice_fusion.5), kind=kOutput, calls=%fused_computation.73.clone.1 | convolution fusion | flops 1090521088 | bytes 20455424 | tf_op jit(solution)/shard_map/while/body/eval_jaxpr/sub | solution.py:59
  205.8 9.3 %fusion.56 = bf16[4,512,128]{1,2,0:T(8,128)(2,1)S(1)} fusion(bf16[2048,4,128]{0,2,1:T(8,128)(2,1)} %get-tuple-element.160, f32[4,512,2048]{2,1,0:T(8,128)} %get-tuple-element.136, f32[4,512]{1,0:T(4,128)S(1)} %get-tuple-element.137), kind=kOutput, calls=%fused_computation.11.clone.1 | convolution fusion | flops 1082392576 | bytes 19406848 | tf_op jit(solution)/shard_map/while/body/eval_jaxpr/hqk,khd->qhd/dot_general | solution.py:61
  219.0 11.0 %fusion.55 = (f32[4,512]{1,0:T(4,128)S(1)}, f32[4,512,2048]{2,1,0:T(8,128)}) fusion(pred[512,2048]{1,0:T(8,128)(4,1)S(1)} %broadcast_compare_fusion.2, bf16[2048,4,128]{2,0,1:T(8,128)(2,1)} %get-tuple-element.159, bf16[1,512,4,128]{3,2,1,0:T(4,128)(2,1)} %constant_dynamic-slice_fusion.5), kind=kOutput, calls=%fused_computation.73.clone.1 | convolution fusion | flops 1090521088 | bytes 20455424 | tf_op jit(solution)/shard_map/while/body/eval_jaxpr/sub | solution.py:59
  230.0 9.3 %fusion.56 = bf16[4,512,128]{1,2,0:T(8,128)(2,1)S(1)} fusion(bf16[2048,4,128]{0,2,1:T(8,128)(2,1)} %get-tuple-element.160, f32[4,512,2048]{2,1,0:T(8,128)} %get-tuple-element.136, f32[4,512]{1,0:T(4,128)S(1)} %get-tuple-element.137), kind=kOutput, calls=%fused_computation.11.clone.1 | convolution fusion | flops 1082392576 | bytes 19406848 | tf_op jit(solution)/shard_map/while/body/eval_jaxpr/hqk,khd->qhd/dot_general | solution.py:61
  243.1 11.0 %fusion.55 = (f32[4,512]{1,0:T(4,128)S(1)}, f32[4,512,2048]{2,1,0:T(8,128)}) fusion(pred[512,2048]{1,0:T(8,128)(4,1)S(1)} %broadcast_compare_fusion.2, bf16[2048,4,128]{2,0,1:T(8,128)(2,1)} %get-tuple-element.159, bf16[1,512,4,128]{3,2,1,0:T(4,128)(2,1)} %constant_dynamic-slice_fusion.5), kind=kOutput, calls=%fused_computation.73.clone.1 | convolution fusion | flops 1090521088 | bytes 20455424 | tf_op jit(solution)/shard_map/while/body/eval_jaxpr/sub | solution.py:59
  254.1 9.3 %fusion.56 = bf16[4,512,128]{1,2,0:T(8,128)(2,1)S(1)} fusion(bf16[2048,4,128]{0,2,1:T(8,128)(2,1)} %get-tuple-element.160, f32[4,512,2048]{2,1,0:T(8,128)} %get-tuple-element.136, f32[4,512]{1,0:T(4,128)S(1)} %get-tuple-element.137), kind=kOutput, calls=%fused_computation.11.clone.1 | convolution fusion | flops 1082392576 | bytes 19406848 | tf_op jit(solution)/shard_map/while/body/eval_jaxpr/hqk,khd->qhd/dot_general | solution.py:61
  267.2 11.0 %fusion.55 = (f32[4,512]{1,0:T(4,128)S(1)}, f32[4,512,2048]{2,1,0:T(8,128)}) fusion(pred[512,2048]{1,0:T(8,128)(4,1)S(1)} %broadcast_compare_fusion.2, bf16[2048,4,128]{2,0,1:T(8,128)(2,1)} %get-tuple-element.159, bf16[1,512,4,128]{3,2,1,0:T(4,128)(2,1)} %constant_dynamic-slice_fusion.5), kind=kOutput, calls=%fused_computation.73.clone.1 | convolution fusion | flops 1090521088 | bytes 20455424 | tf_op jit(solution)/shard_map/while/body/eval_jaxpr/sub | solution.py:59
  278.2 9.3 %fusion.56 = bf16[4,512,128]{1,2,0:T(8,128)(2,1)S(1)} fusion(bf16[2048,4,128]{0,2,1:T(8,128)(2,1)} %get-tuple-element.160, f32[4,512,2048]{2,1,0:T(8,128)} %get-tuple-element.136, f32[4,512]{1,0:T(4,128)S(1)} %get-tuple-element.137), kind=kOutput, calls=%fused_computation.11.clone.1 | convolution fusion | flops 1082392576 | bytes 19406848 | tf_op jit(solution)/shard_map/while/body/eval_jaxpr/hqk,khd->qhd/dot_general | solution.py:61
  288.7 31.5 %all_to_all.131 = bf16[16,128,512]{2,1,0:T(8,128)(2,1)S(1)} all-to-all(bf16[16,128,512]{2,1,0:T(8,128)(2,1)} %bitcast.90), channel_id=1, replica_groups=mesh['dp'=16,'seq'=8] {'dp'}, dimensions={0} | all-to-all | bytes 4194304 | tf_op jit(solution)/shard_map/all_to_all | solution.py:104
  323.5 8.4 %all-to-all-start.9 = ((bf16[8,128,512]{2,1,0:T(8,128)(2,1)}), bf16[8,128,512]{2,1,0:T(8,128)(2,1)S(1)}, u32[]{:S(2)}, u32[]{:S(2)}) async-start(bf16[8,128,512]{2,1,0:T(8,128)(2,1)} %bitcast.95), calls=%async_computation.9 | async-start | bytes 2097152 | tf_op jit(solution)/shard_map/all_to_all | solution.py:108
  333.4 13.7 %all-to-all-done.9 = bf16[8,128,512]{2,1,0:T(8,128)(2,1)S(1)} async-done(((bf16[8,128,512]{2,1,0:T(8,128)(2,1)}), bf16[8,128,512]{2,1,0:T(8,128)(2,1)S(1)}, u32[]{:S(2)}, u32[]{:S(2)}) %all-to-all-start.9) | async-done | bytes 1048608 | tf_op jit(solution)/shard_map/all_to_all | solution.py:108
  (71 shorter events, 69.5 us)
Async XLA Ops:
  0.0 332.1 %copy-start = (bf16[256,4096]{1,0:T(8,128)(2,1)S(1)}, bf16[256,4096]{1,0:T(8,128)(2,1)}, u32[]{:S(2)}) copy-start(bf16[256,4096]{1,0:T(8,128)(2,1)} %param.13) | copy-start | bytes 6291460
  1.4 10.5 %all-to-all-start = ((s32[128,8,1]{0,2,1:T(1,128)}), s32[128,8,1]{0,2,1:T(1,128)S(1)}, u32[]{:S(2)}, u32[]{:S(2)}) async-start(s32[128,8,1]{0,2,1:T(1,128)} %broadcast_in_dim.37), calls=%async_computation | async-start | bytes 8192 | tf_op jit(solution)/shard_map/all_to_all | solution.py:84
  18.4 14.0 %all-to-all-start.1 = ((s32[16,128,1]{1,2,0:T(1,128)}), s32[16,128,1]{1,2,0:T(1,128)S(1)}, u32[]{:S(2)}, u32[]{:S(2)}) async-start(s32[16,128,1]{1,2,0:T(1,128)} %bitcast.11), calls=%async_computation.1 | async-start | bytes 16384 | tf_op jit(solution)/shard_map/all_to_all | solution.py:95
  32.4 20.7 %all-to-all-start.4 = ((bf16[128,8,512]{0,2,1:T(8,128)(2,1)}), bf16[128,8,512]{0,2,1:T(8,128)(2,1)S(1)}, u32[]{:S(2)}, u32[]{:S(2)}) async-start(bf16[128,8,512]{0,2,1:T(8,128)(2,1)} %bitcast.88), calls=%async_computation.4 | async-start | bytes 2097152 | tf_op jit(solution)/shard_map/all_to_all | solution.py:89
  53.1 1.0 copy-start.2
  54.1 19.4 %all-to-all-start.6 = ((bf16[128,8,512]{0,2,1:T(8,128)(2,1)}), bf16[128,8,512]{0,2,1:T(8,128)(2,1)S(1)}, u32[]{:S(2)}, u32[]{:S(2)}) async-start(bf16[128,8,512]{0,2,1:T(8,128)(2,1)} %bitcast.89), calls=%async_computation.6 | async-start | bytes 2097152 | tf_op jit(solution)/shard_map/all_to_all | solution.py:90
  73.6 1.0 copy-start.1
  74.5 19.5 %all-to-all-start.2 = ((bf16[128,8,512]{0,2,1:T(8,128)(2,1)}), bf16[128,8,512]{0,2,1:T(8,128)(2,1)S(1)}, u32[]{:S(2)}, u32[]{:S(2)}) async-start(bf16[128,8,512]{0,2,1:T(8,128)(2,1)} %bitcast.87), calls=%async_computation.2 | async-start | bytes 2097152 | tf_op jit(solution)/shard_map/all_to_all | solution.py:88
  94.0 32.7 %all-to-all-start.5 = ((bf16[16,128,512]{1,2,0:T(8,128)(2,1)}), bf16[16,128,512]{1,2,0:T(8,128)(2,1)}, u32[]{:S(2)}, u32[]{:S(2)}) async-start(bf16[16,128,512]{1,2,0:T(8,128)(2,1)} %copy.54), calls=%async_computation.5 | async-start | bytes 4194304 | tf_op jit(solution)/shard_map/all_to_all | solution.py:100
  126.7 29.7 %all-to-all-start.7 = ((bf16[16,128,512]{2,1,0:T(8,128)(2,1)}), bf16[16,128,512]{2,1,0:T(8,128)(2,1)}, u32[]{:S(2)}, u32[]{:S(2)}) async-start(bf16[16,128,512]{2,1,0:T(8,128)(2,1)} %bitcast.92), calls=%async_computation.7 | async-start | bytes 4194304 | tf_op jit(solution)/shard_map/all_to_all | solution.py:100
  156.5 31.7 %all-to-all-start.3 = ((bf16[16,128,512]{2,1,0:T(8,128)(2,1)}), bf16[16,128,512]{2,1,0:T(8,128)(2,1)}, u32[]{:S(2)}, u32[]{:S(2)}) async-start(bf16[16,128,512]{2,1,0:T(8,128)(2,1)} %bitcast.91), calls=%async_computation.3 | async-start | bytes 4194304 | tf_op jit(solution)/shard_map/all_to_all | solution.py:100
  323.5 8.4 %copy-start.5 = (s32[32]{0:T(128)S(1)}, s32[32]{0:T(128)}, u32[]{:S(2)}) copy-start(s32[32]{0:T(128)} %param.12) | copy-start | bytes 388
  323.5 23.5 %all-to-all-start.9 = ((bf16[8,128,512]{2,1,0:T(8,128)(2,1)}), bf16[8,128,512]{2,1,0:T(8,128)(2,1)S(1)}, u32[]{:S(2)}, u32[]{:S(2)}) async-start(bf16[8,128,512]{2,1,0:T(8,128)(2,1)} %bitcast.95), calls=%async_computation.9 | async-start | bytes 2097152 | tf_op jit(solution)/shard_map/all_to_all | solution.py:108
  347.3 1.0 copy-start.3
  347.3 1.0 copy-start.4
where the time goes:
time: 352 us; the launch traced here: 351 us
  matrix products  103 us (29%)
  waiting for transfers between devices  95.6 us (27%)
  local copies, waits for them, and re-layouts  58.7 us (17%)
  starting transfers between devices  51.6 us (15%)
  blocking collectives  31.5 us (9%)
  other arithmetic  9.93 us (3%)
    sub x4, matrix products, one_block(): weights = jnp.exp(scores - row_max)  44.1 us
    all_to_all x3, waiting for transfers between devices, shards(): lax.all_to_all(for_sending(slotted), 'dp', split_axis=0, concat_axis=0, t...  43.5 us
    dot_general x4, matrix products, one_block(): jnp.einsum('hqk,khd->qhd', soft_probs, value_heads, preferred_element_typ...  37.4 us
    all_to_all x1, blocking collectives, shards(): lax.all_to_all(attended, 'dp', split_axis=0, concat_axis=0, tiled=True)  31.5 us
    all_to_all x3, starting transfers between devices, shards(): lax.all_to_all(for_sending(slotted), 'dp', split_axis=0, concat_axis=0, t...  15.4 us
    dot_general x3, matrix products, place_rows(): jnp.dot(place_mask, single, preferred_element_type=jnp.float32)  14.7 us
    all_to_all x1, waiting for transfers between devices, shards(): lax.all_to_all(unslotted, 'seq', split_axis=0, concat_axis=1, tiled=True)  13.7 us
    all_to_all x1, waiting for transfers between devices, shards(): lax.all_to_all(value_rows, 'seq', split_axis=1, concat_axis=0, tiled=True)  12.9 us
  transfers between devices with their start and end apart: 9, of which 9 were waited for; matrix products, arithmetic and copies ran while one was open for 16% of the time, Pallas kernels for 0%

commit v1 on v0

v1 whole, which is shorter than its diff:
```python
import math

import jax
import jax.numpy as jnp
from jax import lax
from jax.experimental import pallas as pl
from jax.experimental.pallas import tpu as pltpu
from jax.sharding import PartitionSpec as P

HEADS = 32
HEAD_DIM = 128
FREQ = 256
SEG_BIN = 2
BINS = 16
SLOTS = 16
ROWS = 128
GROUP = 32
SIDE = 4
CORES = 2
MASKED = 131072.0
AXES = ("dp", "seq")
HALVES = ((1, 2), (0, 3))


def linear(x, y, z, core):
    return (x * SIDE + z) * (SIDE * CORES) + y * CORES + core


def head_groups():
    return [
        [linear(x, y, z, core) for x in range(SIDE) for z in half for y in range(SIDE)]
        for half in HALVES
        for core in range(CORES)
    ]


def exchange(blocks):
    return lax.all_to_all(
        blocks, AXES, 0, 0, tiled=True, axis_index_groups=head_groups()
    )


def every_device():
    return [
        (x, y, z, core)
        for x in range(SIDE)
        for y in range(SIDE)
        for z in range(SIDE)
        for core in range(CORES)
    ]


def from_chip(value):
    return lax.ppermute(
        value, AXES, [(linear(x, y, z, c), linear(x, y, z ^ 1, c)) for x, y, z, c in every_device()]
    )


def from_core(value):
    return lax.ppermute(
        value, AXES, [(linear(x, y, z, c), linear(x, y, z, c ^ 1)) for x, y, z, c in every_device()]
    )


def scale_rows_table(timesteps, w_mod):
    half_freq = FREQ // 2
    frequencies = jnp.exp(-math.log(10000.0) * jnp.arange(half_freq, dtype=jnp.float32) / half_freq)
    angles = timesteps.astype(jnp.float32)[:, None] * frequencies[None, :]
    embedding = jnp.concatenate([jnp.cos(angles), jnp.sin(angles)], axis=1)
    activated = jax.nn.silu(embedding).astype(jnp.bfloat16)
    return jnp.dot(activated, w_mod, preferred_element_type=jnp.float32)


EXTRA = 8


def split_kernel(rows_ref, *refs):
    heads_ref = refs[-1]
    for head in range(HEADS):
        heads_ref[head, 0:ROWS, :] = rows_ref[:, head * HEAD_DIM : (head + 1) * HEAD_DIM]
        if len(refs) == 2:
            heads_ref[head, ROWS : ROWS + EXTRA, :] = refs[0][...]


def split_heads(rows, extra=None):
    operands = [rows] if extra is None else [rows, extra]
    height = ROWS if extra is None else ROWS + EXTRA
    whole = pl.BlockSpec(memory_space=pltpu.VMEM)
    return pl.pallas_call(
        split_kernel,
        in_specs=[whole] * len(operands),
        out_specs=whole,
        out_shape=jax.ShapeDtypeStruct((HEADS, height, HEAD_DIM), rows.dtype),
        cost_estimate=pl.CostEstimate(flops=0, bytes_accessed=2 * 2**20, transcendentals=0),
        name="split_heads",
    )(*operands)


def one_hot(target_row):
    slot = lax.broadcasted_iota(jnp.int32, (BINS * SLOTS, ROWS), 0)
    return (slot == target_row).astype(jnp.float32).astype(jnp.bfloat16)


def id_row(ref, source):
    return ref[source, ROWS : ROWS + EXTRA, :].astype(jnp.float32)[0:1, :].astype(jnp.int32)


def target_row(ids):
    bins = ids >> 1
    hits = lax.broadcasted_iota(jnp.int32, (BINS, ROWS), 0) == bins
    before = lax.broadcasted_iota(jnp.int32, (ROWS, ROWS), 0) < lax.broadcasted_iota(
        jnp.int32, (ROWS, ROWS), 1
    )
    ranks = jnp.dot(
        hits.astype(jnp.float32).astype(jnp.bfloat16),
        before.astype(jnp.float32).astype(jnp.bfloat16),
        preferred_element_type=jnp.float32,
    )
    rank = jnp.sum(jnp.where(hits, ranks, 0.0), axis=0, keepdims=True)
    return bins * SLOTS + rank.astype(jnp.int32)


def sample_marks(ids):
    mark = lax.broadcasted_iota(jnp.int32, (HEAD_DIM, ROWS), 0)
    return (mark == (ids & 1)).astype(jnp.float32).astype(jnp.bfloat16)


SOURCES_STEP = 8


def spread_kernel(kind, id_ref, part_ref, out_ref):
    for source in range(SOURCES_STEP):
        ids = id_row(id_ref, source)
        place = one_hot(target_row(ids))
        slotted = jnp.dot(place, part_ref[source, 0:ROWS, :], preferred_element_type=jnp.float32)
        if kind != "value":
            marked = lax.dot_general(
                place, sample_marks(ids), (((1,), (1,)), ((), ())), preferred_element_type=jnp.float32
            )
            if kind == "key":
                marked = marked * MASKED - MASKED
            slotted = jnp.concatenate([slotted, marked], axis=1)
        out_ref[:, source * SLOTS : (source + 1) * SLOTS, :] = slotted.astype(jnp.bfloat16).reshape(
            BINS, SLOTS, slotted.shape[1]
        )


def spread(kind, key_part, part):
    width = HEAD_DIM if kind == "value" else 2 * HEAD_DIM
    return pl.pallas_call(
        lambda *refs: spread_kernel(kind, *refs),
        grid=(GROUP // SOURCES_STEP,),
        in_specs=[
            pl.BlockSpec((SOURCES_STEP, ROWS + EXTRA, HEAD_DIM), lambda i: (i, 0, 0)),
            pl.BlockSpec((SOURCES_STEP,) + part.shape[1:], lambda i: (i, 0, 0)),
        ],
        out_specs=pl.BlockSpec((BINS, SOURCES_STEP * SLOTS, width), lambda i: (0, i, 0)),
        out_shape=jax.ShapeDtypeStruct((BINS, GROUP * SLOTS, width), jnp.bfloat16),
        compiler_params=pltpu.CompilerParams(vmem_limit_bytes=32 * 2**20),
        cost_estimate=pl.CostEstimate(
            flops=2 * GROUP * BINS * SLOTS * ROWS * width,
            bytes_accessed=2**20 + BINS * GROUP * SLOTS * width * 2,
            transcendentals=0,
        ),
        name="spread_" + kind,
    )(key_part, part)


QUERY_TILE = 512


def attend_kernel(id_ref, query_ref, *refs):
    key_refs, value_refs = refs[:4], refs[4:8]
    out_ref, slots_ref = refs[8:]
    step = pl.program_id(0)
    score_scale = 1.0 / math.sqrt(HEAD_DIM)
    length = GROUP * SLOTS
    ones = jnp.ones((length, HEAD_DIM), jnp.bfloat16)
    for tile in range(length // QUERY_TILE):
        rows = slice(tile * QUERY_TILE, (tile + 1) * QUERY_TILE)
        query = query_ref[0, rows, :]
        scores = [
            lax.dot_general(
                query, key_ref[0], (((1,), (1,)), ((), ())), preferred_element_type=jnp.float32
            )
            for key_ref in key_refs
        ]
        row_max = jnp.max(
            jnp.maximum(jnp.maximum(scores[0], scores[1]), jnp.maximum(scores[2], scores[3])),
            axis=1,
            keepdims=True,
        )
        total = None
        for part, value_ref in zip(scores, value_refs):
            weights = jnp.exp((part - row_max) * score_scale).astype(jnp.bfloat16)
            wide = jnp.concatenate([value_ref[0], ones], axis=1)
            product = jnp.dot(weights, wide, preferred_element_type=jnp.float32)
            total = product if total is None else total + product
        slots_ref[step, rows, :] = (total[:, :HEAD_DIM] / total[:, HEAD_DIM:]).astype(jnp.bfloat16)

    @pl.when(step == BINS - 1)
    def _():
        for source in range(GROUP):
            place = one_hot(target_row(id_row(id_ref, source)))
            held = slots_ref[:, source * SLOTS : (source + 1) * SLOTS, :].reshape(
                BINS * SLOTS, HEAD_DIM
            )
            out_ref[source] = lax.dot_general(
                place, held, (((0,), (0,)), ((), ())), preferred_element_type=jnp.float32
            ).astype(jnp.bfloat16)


def attend(key_part, query, keys, values):
    length = GROUP * SLOTS
    wide = pl.BlockSpec((1, length, 2 * HEAD_DIM), lambda i: (i, 0, 0))
    narrow = pl.BlockSpec((1, length, HEAD_DIM), lambda i: (i, 0, 0))
    pairs = BINS * length * length * len(keys)
    return pl.pallas_call(
        attend_kernel,
        grid=(BINS,),
        in_specs=[pl.BlockSpec((GROUP, ROWS + EXTRA, HEAD_DIM), lambda i: (0, 0, 0)), wide]
        + [wide] * len(keys)
        + [narrow] * len(values),
        out_specs=pl.BlockSpec((GROUP, ROWS, HEAD_DIM), lambda i: (0, 0, 0)),
        out_shape=jax.ShapeDtypeStruct((GROUP, ROWS, HEAD_DIM), jnp.bfloat16),
        scratch_shapes=[pltpu.VMEM((BINS, length, HEAD_DIM), jnp.bfloat16)],
        compiler_params=pltpu.CompilerParams(vmem_limit_bytes=48 * 2**20),
        cost_estimate=pl.CostEstimate(
            flops=8 * pairs * HEAD_DIM, bytes_accessed=28 * 2**20, transcendentals=pairs
        ),
        name="attend",
    )(key_part, query, *keys, *values)


def finish_kernel(heads_ref, scale_ref, out_ref):
    for head in range(HEADS):
        columns = slice(head * HEAD_DIM, (head + 1) * HEAD_DIM)
        out_ref[:, columns] = (
            heads_ref[head].astype(jnp.float32) * (1.0 + scale_ref[:, columns])
        ).astype(jnp.bfloat16)


def finish(heads, row_scales):
    whole = pl.BlockSpec(memory_space=pltpu.VMEM)
    return pl.pallas_call(
        finish_kernel,
        in_specs=[whole, whole],
        out_specs=whole,
        out_shape=jax.ShapeDtypeStruct((ROWS, HEADS * HEAD_DIM), jnp.bfloat16),
        cost_estimate=pl.CostEstimate(flops=2**20, bytes_accessed=4 * 2**20, transcendentals=0),
        name="finish",
    )(heads, row_scales)


def shards(query_rows, key_rows, value_rows, seg_ids, timesteps, w_mod):
    def gathered(own):
        chip = from_chip(own)
        return own, chip, from_core(own), from_core(chip)

    id_rows = jnp.broadcast_to(seg_ids.astype(jnp.bfloat16)[None, :], (EXTRA, ROWS))
    key_parts = gathered(exchange(split_heads(key_rows, id_rows)))
    value_parts = gathered(exchange(split_heads(value_rows)))
    own_query = exchange(split_heads(query_rows))

    keys = [spread("key", p, p) for p in key_parts]
    values = [spread("value", k, p) for k, p in zip(key_parts, value_parts)]
    query = spread("query", key_parts[0], own_query)
    home = exchange(attend(key_parts[0], query, keys, values))

    scale_table = scale_rows_table(timesteps, w_mod)
    lookup = (
        seg_ids[:, None] == jnp.arange(scale_table.shape[0], dtype=jnp.int32)[None, :]
    ).astype(jnp.float32)
    row_scales = jnp.dot(
        lookup, scale_table, precision=lax.Precision.HIGHEST, preferred_element_type=jnp.float32
    )
    return finish(home, row_scales)


def solution(mesh):
    placed = (
        P(("dp", "seq"), None),
        P(("dp", "seq"), None),
        P(("dp", "seq"), None),
        P(("dp", "seq")),
        P(),
        P(),
    )
    return jax.shard_map(
        shards, mesh=mesh, in_specs=placed, out_specs=P(("dp", "seq"), None), check_vma=False
    )
```

time: 352 us -> 236 us (0.67)
  Pallas kernels: 0 us -> 111 us
  matrix products: 103 us -> 2.81 us
  local copies, waits for them, and re-layouts: 58.7 us -> 17.8 us
  waiting for transfers between devices: 95.6 us -> 62.1 us
  blocking collectives: 31.5 us -> 0 us
  starting transfers between devices: 51.6 us -> 39.9 us
  other arithmetic: 9.93 us -> 0.96 us
    pallas_call x0 -> x14, Pallas kernels: none -> 111 us  [the longest x9 55.5 us: spread(): pl.pallas_call(lambda *refs: spread_kernel(kind, *refs), grid=(GROUP // S...]
    dot_general x8 -> x0, matrix products: 55.4 us -> none  [the longest x4 37.4 us: one_block(): jnp.einsum('hqk,khd->qhd', soft_probs, value_heads, preferred_element_typ...]
    all_to_all x9 -> x4, waiting for transfers between devices: 95.6 us -> 43.7 us  [exchange(): lax.all_to_all(blocks, AXES, 0, 0, tiled=True, axis_index_groups=head_gro...]
    sub x4 -> x0, matrix products: 44.1 us -> none  [one_block(): weights = jnp.exp(scores - row_max)]
    all_to_all x1 -> x0, blocking collectives: 31.5 us -> none  [shards(): lax.all_to_all(attended, 'dp', split_axis=0, concat_axis=0, tiled=True)]
    all_to_all x9 -> x4, starting transfers between devices: 51.6 us -> 31.2 us  [exchange(): lax.all_to_all(blocks, AXES, 0, 0, tiled=True, axis_index_groups=head_gro...]
    ppermute x0 -> x6, waiting for transfers between devices: none -> 18.4 us  [the longest x2 18.4 us: from_chip(): lax.ppermute(value, AXES, [(linear(x, y, z, c), linear(x, y, z ^ 1, c)) f...]
    reshape x5 -> x0, local copies, waits for them, and re-layouts: 16.4 us -> none  [the longest x2 8.28 us: attend_slots(): value_heads = value_part.reshape(length, head_count, HEAD_DIM)]
  transfers between devices with their start and end apart: 9 -> 10, of which waited for: 9 -> 4; matrix products, arithmetic and copies ran while one was open for 16% -> 1% of each run, Pallas kernels for 0% -> 24%
where the time goes in v1:
time: 236 us; the launch traced here: 235 us
  Pallas kernels  111 us (47%)
  waiting for transfers between devices  62.1 us (26%)
  starting transfers between devices  39.9 us (17%)
  local copies, waits for them, and re-layouts  17.8 us (8%)
  matrix products  2.81 us (1%)
    pallas_call x9, Pallas kernels, spread(): pl.pallas_call(lambda *refs: spread_kernel(kind, *refs), grid=(GROUP // S...  55.5 us
    pallas_call x1, Pallas kernels, attend(): pl.pallas_call(attend_kernel, grid=(BINS,), in_specs=[pl.BlockSpec((GROUP...  45.6 us
    all_to_all x4, waiting for transfers between devices, exchange(): lax.all_to_all(blocks, AXES, 0, 0, tiled=True, axis_index_groups=head_gro...  43.7 us
    all_to_all x4, starting transfers between devices, exchange(): lax.all_to_all(blocks, AXES, 0, 0, tiled=True, axis_index_groups=head_gro...  31.2 us
    ppermute x2, waiting for transfers between devices, from_chip(): lax.ppermute(value, AXES, [(linear(x, y, z, c), linear(x, y, z ^ 1, c)) f...  18.4 us
    unnamed x30, local copies, waits for them, and re-layouts  17.2 us
    ppermute x4, starting transfers between devices, from_core(): lax.ppermute(value, AXES, [(linear(x, y, z, c), linear(x, y, z, c ^ 1)) f...  8.62 us
    pallas_call x3, Pallas kernels, split_heads(): pl.pallas_call(split_kernel, in_specs=[whole] * len(operands), out_specs=...  7.18 us
  transfers between devices with their start and end apart: 10, of which 4 were waited for; matrix products, arithmetic and copies ran while one was open for 1% of the time, Pallas kernels for 24%

profile of v1, /device:TPU:1, one launch (start us, length us, event | category | flops | bytes accessed | tf_op | source)
XLA Modules:
  0.0 235.3 jit_solution(6824758787403664886)
XLA Ops:
  1.4 2.4 %split_heads.3 = bf16[32,136,128]{2,1,0:T(8,128)(2,1)} custom-call(bf16[128,4096]{1,0:T(8,128)(2,1)} %rows_ref.3, bf16[8,128]{1,0:T(8,128)(2,1)} %broadcast_in_dim.2.refs_0_), custom_call_target="tpu_custom_call" | custom-call | bytes 2097152 | tf_op jit(solution)/shard_map/split_heads/pallas_call | solution.py:89
  3.8 11.3 %all-to-all-start = ((bf16[32,136,128]{2,1,0:T(8,128)(2,1)}), bf16[32,136,128]{2,1,0:T(8,128)(2,1)S(1)}, u32[]{:S(2)}, u32[]{:S(2)}) async-start(bf16[32,136,128]{2,1,0:T(8,128)(2,1)} %split_heads.3), calls=%async_computation | async-start | bytes 2228224 | tf_op jit(solution)/shard_map/all_to_all | solution.py:38
  15.2 2.4 %split_heads.5 = bf16[32,128,128]{2,1,0:T(8,128)(2,1)} custom-call(bf16[128,4096]{1,0:T(8,128)(2,1)} %rows_ref.5), custom_call_target="tpu_custom_call" | custom-call | bytes 2097152 | tf_op jit(solution)/shard_map/split_heads/pallas_call | solution.py:89
  17.5 14.2 %all-to-all-done.refs_0_.refs_1_.id_ref = bf16[32,136,128]{2,1,0:T(8,128)(2,1)S(1)} async-done(((bf16[32,136,128]{2,1,0:T(8,128)(2,1)}), bf16[32,136,128]{2,1,0:T(8,128)(2,1)S(1)}, u32[]{:S(2)}, u32[]{:S(2)}) %all-to-all-start) | async-done | bytes 1114144 | tf_op jit(solution)/shard_map/all_to_all | solution.py:38
  31.8 6.2 %all-to-all-start.2 = ((bf16[32,128,128]{2,1,0:T(8,128)(2,1)}), bf16[32,128,128]{2,1,0:T(8,128)(2,1)}, u32[]{:S(2)}, u32[]{:S(2)}) async-start(bf16[32,128,128]{2,1,0:T(8,128)(2,1)} %split_heads.5), calls=%async_computation.2 | async-start | bytes 2097152 | tf_op jit(solution)/shard_map/all_to_all | solution.py:38
  38.0 15.5 %all-to-all-done.2.refs_1_ = bf16[32,128,128]{2,1,0:T(8,128)(2,1)} async-done(((bf16[32,128,128]{2,1,0:T(8,128)(2,1)}), bf16[32,128,128]{2,1,0:T(8,128)(2,1)}, u32[]{:S(2)}, u32[]{:S(2)}) %all-to-all-start.2) | async-done | bytes 1048608 | tf_op jit(solution)/shard_map/all_to_all | solution.py:38
  53.5 3.1 %collective-permute-start.1 = (bf16[32,136,128]{2,1,0:T(8,128)(2,1)S(1)}, bf16[32,136,128]{2,1,0:T(8,128)(2,1)}, u32[]{:S(2)}, u32[]{:S(2)}) collective-permute-start(bf16[32,136,128]{2,1,0:T(8,128)(2,1)S(1)} %all-to-all-done.refs_0_.refs_1_.id_ref), channel_id=1, source_target_pairs={{0,1},{1,0},{8,9},{9,8},{16,17},{17,16},{24,25},{25,24},{2,3},{3,2... | collective-permute-start | bytes 3342344 | tf_op jit(solution)/shard_map/ppermute | solution.py:60
  56.6 2.4 %split_heads.4 = bf16[32,128,128]{2,1,0:T(8,128)(2,1)} custom-call(bf16[128,4096]{1,0:T(8,128)(2,1)} %rows_ref.4), custom_call_target="tpu_custom_call" | custom-call | bytes 2097152 | tf_op jit(solution)/shard_map/split_heads/pallas_call | solution.py:89
  58.9 4.7 %all-to-all-start.1 = ((bf16[32,128,128]{2,1,0:T(8,128)(2,1)}), bf16[32,128,128]{2,1,0:T(8,128)(2,1)}, u32[]{:S(2)}, u32[]{:S(2)}) async-start(bf16[32,128,128]{2,1,0:T(8,128)(2,1)} %split_heads.4), calls=%async_computation.1 | async-start | bytes 2097152 | tf_op jit(solution)/shard_map/all_to_all | solution.py:38
  63.7 3.2 %collective-permute-start.2 = (bf16[32,136,128]{2,1,0:T(8,128)(2,1)}, bf16[32,136,128]{2,1,0:T(8,128)(2,1)}, u32[]{:S(2)}, u32[]{:S(2)}) collective-permute-start(bf16[32,136,128]{2,1,0:T(8,128)(2,1)} %collective-permute-done.refs_0_.refs_1_), channel_id=1, source_target_pairs={{0,1},{1,0},{8,9},{9,8},{16,17},{17,16},{24,25},{25,24},{2,3},{3,2... | collective-permute-start | bytes 3342344 | tf_op jit(solution)/shard_map/ppermute | solution.py:60
  66.9 18.4 %collective-permute-done.3.refs_1_ = bf16[32,128,128]{2,1,0:T(8,128)(2,1)} collective-permute-done((bf16[32,128,128]{2,1,0:T(8,128)(2,1)}, bf16[32,128,128]{2,1,0:T(8,128)(2,1)}, u32[]{:S(2)}, u32[]{:S(2)}) %collective-permute-start.3) | collective-permute-done | bytes 1048608 | tf_op jit(solution)/shard_map/ppermute | solution.py:54
  85.3 2.2 collective-permute-start.5
  87.6 4.5 %spread_value.4.refs_4_ = bf16[16,512,128]{2,1,0:T(8,128)(2,1)S(1)} custom-call(bf16[32,136,128]{2,1,0:T(8,128)(2,1)S(1)} %all-to-all-done.refs_0_.refs_1_.id_ref, bf16[32,128,128]{2,1,0:T(8,128)(2,1)} %all-to-all-done.2.refs_1_), custom_call_target="tpu_custom_call" | custom-call | flops 268435456 | bytes 3145728 | tf_op jit(solution)/shard_map/spread_value/pallas_call | solution.py:150
  93.5 6.4 %spread_key.4.refs_0_ = bf16[16,512,256]{2,1,0:T(8,128)(2,1)S(1)} custom-call(bf16[32,136,128]{2,1,0:T(8,128)(2,1)S(1)} %all-to-all-done.refs_0_.refs_1_.id_ref, bf16[32,136,128]{2,1,0:T(8,128)(2,1)S(1)} %all-to-all-done.refs_0_.refs_1_.id_ref), custom_call_target="tpu_custom_call" | custom-call | flops 536870912 | bytes 5242880 | tf_op jit(solution)/shard_map/spread_key/pallas_call | solution.py:150
  99.9 1.9 copy-done.2
  101.9 7.4 %spread_query.1.query_ref = bf16[16,512,256]{2,1,0:T(8,128)(2,1)S(1)} custom-call(bf16[32,136,128]{2,1,0:T(8,128)(2,1)S(1)} %all-to-all-done.refs_0_.refs_1_.id_ref, bf16[32,128,128]{2,1,0:T(8,128)(2,1)} %all-to-all-done.1.refs_1_), custom_call_target="tpu_custom_call" | custom-call | flops 536870912 | bytes 5242880 | tf_op jit(solution)/shard_map/spread_query/pallas_call | solution.py:150
  109.3 2.0 copy-done.1
  111.3 4.7 %spread_value.5.refs_5_ = bf16[16,512,128]{2,1,0:T(8,128)(2,1)S(1)} custom-call(bf16[32,136,128]{2,1,0:T(8,128)(2,1)} %collective-permute-done.refs_0_.refs_1_, bf16[32,128,128]{2,1,0:T(8,128)(2,1)} %collective-permute-done.3.refs_1_), custom_call_target="tpu_custom_call" | custom-call | flops 268435456 | bytes 3145728 | tf_op jit(solution)/shard_map/spread_value/pallas_call | solution.py:150
  116.1 1.4 copy-done.8
  117.5 4.7 %spread_value.6.refs_6_ = bf16[16,512,128]{2,1,0:T(8,128)(2,1)S(1)} custom-call(bf16[32,136,128]{2,1,0:T(8,128)(2,1)} %collective-permute-done.1.refs_0_.refs_1_, bf16[32,128,128]{2,1,0:T(8,128)(2,1)} %collective-permute-done.4.refs_1_), custom_call_target="tpu_custom_call" | custom-call | flops 268435456 | bytes 3145728 | tf_op jit(solution)/shard_map/spread_value/pallas_call | solution.py:150
  123.6 7.5 %spread_key.5.refs_1_ = bf16[16,512,256]{2,1,0:T(8,128)(2,1)S(1)} custom-call(bf16[32,136,128]{2,1,0:T(8,128)(2,1)} %collective-permute-done.refs_0_.refs_1_, bf16[32,136,128]{2,1,0:T(8,128)(2,1)} %collective-permute-done.refs_0_.refs_1_), custom_call_target="tpu_custom_call" | custom-call | flops 536870912 | bytes 5242880 | tf_op jit(solution)/shard_map/spread_key/pallas_call | solution.py:150
  131.1 2.0 copy-done.3
  133.1 7.6 %spread_key.6.refs_2_ = bf16[16,512,256]{2,1,0:T(8,128)(2,1)S(1)} custom-call(bf16[32,136,128]{2,1,0:T(8,128)(2,1)} %collective-permute-done.1.refs_0_.refs_1_, bf16[32,136,128]{2,1,0:T(8,128)(2,1)} %collective-permute-done.1.refs_0_.refs_1_), custom_call_target="tpu_custom_call" | custom-call | flops 536870912 | bytes 5242880 | tf_op jit(solution)/shard_map/spread_key/pallas_call | solution.py:150
  140.7 1.9 copy-done.4
  142.7 7.6 %spread_key.7.refs_3_ = bf16[16,512,256]{2,1,0:T(8,128)(2,1)S(1)} custom-call(bf16[32,136,128]{2,1,0:T(8,128)(2,1)} %collective-permute-done.2.refs_0_.refs_1_, bf16[32,136,128]{2,1,0:T(8,128)(2,1)} %collective-permute-done.2.refs_0_.refs_1_), custom_call_target="tpu_custom_call" | custom-call | flops 536870912 | bytes 5242880 | tf_op jit(solution)/shard_map/spread_key/pallas_call | solution.py:150
  150.3 1.9 copy-done.5
  152.2 4.9 %spread_value.7.refs_7_ = bf16[16,512,128]{2,1,0:T(8,128)(2,1)S(1)} custom-call(bf16[32,136,128]{2,1,0:T(8,128)(2,1)} %collective-permute-done.2.refs_0_.refs_1_, bf16[32,128,128]{2,1,0:T(8,128)(2,1)} %collective-permute-done.5.refs_1_), custom_call_target="tpu_custom_call" | custom-call | flops 268435456 | bytes 3145728 | tf_op jit(solution)/shard_map/spread_value/pallas_call | solution.py:150
  158.5 45.6 %attend.1 = bf16[32,128,128]{2,1,0:T(8,128)(2,1)S(1)} custom-call(bf16[32,136,128]{2,1,0:T(8,128)(2,1)S(1)} %all-to-all-done.refs_0_.refs_1_.id_ref, bf16[16,512,256]{2,1,0:T(8,128)(2,1)} %copy-done.1, bf16[16,512,256]{2,1,0:T(8,128)(2,1)} %copy-done.2, bf16[16,512,256]{2,1,0:T(8,128)(2,1)} %copy-done.3, bf16[16,512,256]{2,1,0:T(8,128)(2,1)} %copy-done.4, ...), custom_call_target="tpu_custom_call" | custom-call | flops 17179869184 | bytes 29360128 | tf_op jit(solution)/shard_map/attend/pallas_call | solution.py:218
  205.0 9.0 %all-to-all-start.3 = ((bf16[32,128,128]{2,1,0:T(8,128)(2,1)}), bf16[32,128,128]{2,1,0:T(8,128)(2,1)S(1)}, u32[]{:S(2)}, u32[]{:S(2)}) async-start(bf16[32,128,128]{2,1,0:T(8,128)(2,1)} %copy-done.11), calls=%async_computation.3 | async-start | bytes 2097152 | tf_op jit(solution)/shard_map/all_to_all | solution.py:38
  214.7 2.4 %fusion.scale_ref = f32[128,4096]{1,0:T(8,128)} fusion(f32[32,4096]{1,0:T(8,128)S(1)} %fusion.2, s32[128]{0:T(128)S(1)} %copy-done.13), kind=kOutput, calls=%fused_computation.1 | convolution fusion | flops 201330688 | bytes 2621952 | tf_op jit(solution)/shard_map/dot_general | solution.py:274
  217.1 14.0 %all-to-all-done.3.heads_ref = bf16[32,128,128]{2,1,0:T(8,128)(2,1)S(1)} async-done(((bf16[32,128,128]{2,1,0:T(8,128)(2,1)}), bf16[32,128,128]{2,1,0:T(8,128)(2,1)S(1)}, u32[]{:S(2)}, u32[]{:S(2)}) %all-to-all-start.3) | async-done | bytes 1048608 | tf_op jit(solution)/shard_map/all_to_all | solution.py:38
  232.1 3.2 %finish.1 = bf16[128,4096]{1,0:T(8,128)(2,1)} custom-call(bf16[32,128,128]{2,1,0:T(8,128)(2,1)} %copy-done.12, f32[128,4096]{1,0:T(8,128)} %fusion.scale_ref), custom_call_target="tpu_custom_call" | custom-call | flops 1048576 | bytes 4194304 | tf_op jit(solution)/shard_map/finish/pallas_call | solution.py:245
  (39 shorter events, 8.2 us)
Async XLA Ops:
  0.0 214.2 %copy-start = (bf16[256,4096]{1,0:T(8,128)(2,1)S(1)}, bf16[256,4096]{1,0:T(8,128)(2,1)}, u32[]{:S(2)}) copy-start(bf16[256,4096]{1,0:T(8,128)(2,1)} %param.11) | copy-start | bytes 6291460
  3.8 27.9 %all-to-all-start = ((bf16[32,136,128]{2,1,0:T(8,128)(2,1)}), bf16[32,136,128]{2,1,0:T(8,128)(2,1)S(1)}, u32[]{:S(2)}, u32[]{:S(2)}) async-start(bf16[32,136,128]{2,1,0:T(8,128)(2,1)} %split_heads.3), calls=%async_computation | async-start | bytes 2228224 | tf_op jit(solution)/shard_map/all_to_all | solution.py:38
  31.8 21.7 %all-to-all-start.2 = ((bf16[32,128,128]{2,1,0:T(8,128)(2,1)}), bf16[32,128,128]{2,1,0:T(8,128)(2,1)}, u32[]{:S(2)}, u32[]{:S(2)}) async-start(bf16[32,128,128]{2,1,0:T(8,128)(2,1)} %split_heads.5), calls=%async_computation.2 | async-start | bytes 2097152 | tf_op jit(solution)/shard_map/all_to_all | solution.py:38
  37.9 25.8 %collective-permute-start = (bf16[32,136,128]{2,1,0:T(8,128)(2,1)S(1)}, bf16[32,136,128]{2,1,0:T(8,128)(2,1)}, u32[]{:S(2)}, u32[]{:S(2)}) collective-permute-start(bf16[32,136,128]{2,1,0:T(8,128)(2,1)S(1)} %all-to-all-done.refs_0_.refs_1_.id_ref), channel_id=1, source_target_pairs={{0,8},{1,9},{8,0},{9,1},{16,24},{17,25},{24,16},{25,17},{2,10},{3,... | collective-permute-start | bytes 3342344 | tf_op jit(solution)/shard_map/ppermute | solution.py:54
  53.5 31.9 %collective-permute-start.3 = (bf16[32,128,128]{2,1,0:T(8,128)(2,1)}, bf16[32,128,128]{2,1,0:T(8,128)(2,1)}, u32[]{:S(2)}, u32[]{:S(2)}) collective-permute-start(bf16[32,128,128]{2,1,0:T(8,128)(2,1)} %all-to-all-done.2.refs_1_), channel_id=1, source_target_pairs={{0,8},{1,9},{8,0},{9,1},{16,24},{17,25},{24,16},{25,17},{2,10},{3,... | collective-permute-start | bytes 3145736 | tf_op jit(solution)/shard_map/ppermute | solution.py:54
  53.5 64.0 %collective-permute-start.1 = (bf16[32,136,128]{2,1,0:T(8,128)(2,1)S(1)}, bf16[32,136,128]{2,1,0:T(8,128)(2,1)}, u32[]{:S(2)}, u32[]{:S(2)}) collective-permute-start(bf16[32,136,128]{2,1,0:T(8,128)(2,1)S(1)} %all-to-all-done.refs_0_.refs_1_.id_ref), channel_id=1, source_target_pairs={{0,1},{1,0},{8,9},{9,8},{16,17},{17,16},{24,25},{25,24},{2,3},{3,2... | collective-permute-start | bytes 3342344 | tf_op jit(solution)/shard_map/ppermute | solution.py:60
  58.9 43.0 %all-to-all-start.1 = ((bf16[32,128,128]{2,1,0:T(8,128)(2,1)}), bf16[32,128,128]{2,1,0:T(8,128)(2,1)}, u32[]{:S(2)}, u32[]{:S(2)}) async-start(bf16[32,128,128]{2,1,0:T(8,128)(2,1)} %split_heads.4), calls=%async_computation.1 | async-start | bytes 2097152 | tf_op jit(solution)/shard_map/all_to_all | solution.py:38
  63.6 53.9 %collective-permute-start.4 = (bf16[32,128,128]{2,1,0:T(8,128)(2,1)}, bf16[32,128,128]{2,1,0:T(8,128)(2,1)}, u32[]{:S(2)}, u32[]{:S(2)}) collective-permute-start(bf16[32,128,128]{2,1,0:T(8,128)(2,1)} %all-to-all-done.2.refs_1_), channel_id=1, source_target_pairs={{0,1},{1,0},{8,9},{9,8},{16,17},{17,16},{24,25},{25,24},{2,3},{3,2... | collective-permute-start | bytes 3145736 | tf_op jit(solution)/shard_map/ppermute | solution.py:60
  63.7 79.0 %collective-permute-start.2 = (bf16[32,136,128]{2,1,0:T(8,128)(2,1)}, bf16[32,136,128]{2,1,0:T(8,128)(2,1)}, u32[]{:S(2)}, u32[]{:S(2)}) collective-permute-start(bf16[32,136,128]{2,1,0:T(8,128)(2,1)} %collective-permute-done.refs_0_.refs_1_), channel_id=1, source_target_pairs={{0,1},{1,0},{8,9},{9,8},{16,17},{17,16},{24,25},{25,24},{2,3},{3,2... | collective-permute-start | bytes 3342344 | tf_op jit(solution)/shard_map/ppermute | solution.py:60
  85.3 66.9 %collective-permute-start.5 = (bf16[32,128,128]{2,1,0:T(8,128)(2,1)}, bf16[32,128,128]{2,1,0:T(8,128)(2,1)}, u32[]{:S(2)}, u32[]{:S(2)}) collective-permute-start(bf16[32,128,128]{2,1,0:T(8,128)(2,1)} %collective-permute-done.3.refs_1_), channel_id=1, source_target_pairs={{0,1},{1,0},{8,9},{9,8},{16,17},{17,16},{24,25},{25,24},{2,3},{3,2... | collective-permute-start | bytes 3145736 | tf_op jit(solution)/shard_map/ppermute | solution.py:60
  92.1 1.4 copy-start.6
  99.9 2.0 copy-start.2
  109.3 2.0 copy-start.1
  116.1 1.4 copy-start.8
  122.2 1.4 copy-start.9
  131.1 2.0 copy-start.3
  140.7 1.9 copy-start.4
  150.3 2.0 copy-start.5
  152.2 6.3 %copy-start.7 = (bf16[16,512,128]{2,1,0:T(8,128)(2,1)S(1)}, bf16[16,512,128]{2,1,0:T(8,128)(2,1)}, u32[]{:S(2)}) copy-start(bf16[16,512,128]{2,1,0:T(8,128)(2,1)} %copy-done.6) | copy-start | bytes 6291460
  157.1 1.3 copy-start.10
  204.1 1.0 copy-start.11
  205.0 9.0 %copy-start.14 = (s32[32]{0:T(128)S(1)}, s32[32]{0:T(128)}, u32[]{:S(2)}) copy-start(s32[32]{0:T(128)} %param.10) | copy-start | bytes 388
  205.0 9.7 %copy-start.13 = (s32[128]{0:T(128)S(1)}, s32[128]{0:T(128)}, u32[]{:S(2)}) copy-start(s32[128]{0:T(128)} %param.9) | copy-start | bytes 1540
  205.0 26.1 %all-to-all-start.3 = ((bf16[32,128,128]{2,1,0:T(8,128)(2,1)}), bf16[32,128,128]{2,1,0:T(8,128)(2,1)S(1)}, u32[]{:S(2)}, u32[]{:S(2)}) async-start(bf16[32,128,128]{2,1,0:T(8,128)(2,1)} %copy-done.11), calls=%async_computation.3 | async-start | bytes 2097152 | tf_op jit(solution)/shard_map/all_to_all | solution.py:38
  231.1 1.0 copy-start.12

commit v2 on v1

v2 whole, which is shorter than its diff:
```python
import math

import jax
import jax.numpy as jnp
from jax import lax
from jax.experimental import pallas as pl
from jax.experimental.pallas import tpu as pltpu
from jax.sharding import PartitionSpec as P

HEADS = 32
HEAD_DIM = 128
FREQ = 256
SEG_BIN = 2
BINS = 16
ROWS = 128
GROUP = 32
SIDE = 4
CORES = 2
MASKED = 131072.0
AXES = ("dp", "seq")
HALVES = ((1, 2), (0, 3))


def linear(x, y, z, core):
    return (x * SIDE + z) * (SIDE * CORES) + y * CORES + core


def head_groups():
    return [
        [linear(x, y, z, core) for x in range(SIDE) for z in half for y in range(SIDE)]
        for half in HALVES
        for core in range(CORES)
    ]


def exchange(blocks):
    return lax.all_to_all(
        blocks, AXES, 0, 0, tiled=True, axis_index_groups=head_groups()
    )


def every_device():
    return [
        (x, y, z, core)
        for x in range(SIDE)
        for y in range(SIDE)
        for z in range(SIDE)
        for core in range(CORES)
    ]


def from_chip(value):
    return lax.ppermute(
        value, AXES, [(linear(x, y, z, c), linear(x, y, z ^ 1, c)) for x, y, z, c in every_device()]
    )


def from_core(value):
    return lax.ppermute(
        value, AXES, [(linear(x, y, z, c), linear(x, y, z, c ^ 1)) for x, y, z, c in every_device()]
    )


def scale_rows_table(timesteps, w_mod):
    half_freq = FREQ // 2
    frequencies = jnp.exp(-math.log(10000.0) * jnp.arange(half_freq, dtype=jnp.float32) / half_freq)
    angles = timesteps.astype(jnp.float32)[:, None] * frequencies[None, :]
    embedding = jnp.concatenate([jnp.cos(angles), jnp.sin(angles)], axis=1)
    activated = jax.nn.silu(embedding).astype(jnp.bfloat16)
    return jnp.dot(activated, w_mod, preferred_element_type=jnp.float32)


EXTRA = 8


def split_kernel(rows_ref, *refs):
    heads_ref = refs[-1]
    if len(refs) == 2:
        ids = jnp.broadcast_to(refs[0][...].astype(jnp.float32), (EXTRA, ROWS)).astype(jnp.bfloat16)
    for head in range(HEADS):
        heads_ref[head, 0:ROWS, :] = rows_ref[:, head * HEAD_DIM : (head + 1) * HEAD_DIM]
        if len(refs) == 2:
            heads_ref[head, ROWS : ROWS + EXTRA, :] = ids


def split_heads(rows, extra=None):
    operands = [rows] if extra is None else [rows, extra]
    height = ROWS if extra is None else ROWS + EXTRA
    whole = pl.BlockSpec(memory_space=pltpu.VMEM)
    return pl.pallas_call(
        split_kernel,
        in_specs=[whole] * len(operands),
        out_specs=whole,
        out_shape=jax.ShapeDtypeStruct((HEADS, height, HEAD_DIM), rows.dtype),
        cost_estimate=pl.CostEstimate(flops=0, bytes_accessed=2 * 2**20, transcendentals=0),
        name="split_heads",
    )(*operands)


TILE = 16
PAIR = 2
WINDOW = 3 * TILE
PLACES = GROUP * ROWS
CHUNK = 128
LENGTH = PLACES + CHUNK
KEY_TILE = 256
SIZES = ((320, 1152), (320, 1408), (448, 1408), (528, 2304))
QUERY_LENGTH = GROUP * ROWS + SIZES[-1][0]
HELD = SIZES[-1][1] + KEY_TILE


def as_bf16(mask):
    return mask.astype(jnp.float32).astype(jnp.bfloat16)


def iota(shape, dimension):
    return lax.broadcasted_iota(jnp.int32, shape, dimension)


def plan(ids):
    bins = ids >> 1
    hits = [(bins == b).astype(jnp.float32) for b in range(BINS)]
    lane = iota((GROUP, ROWS), 1)
    counts = jnp.zeros((GROUP, ROWS), jnp.float32)
    for b in range(BINS):
        counts = jnp.where(lane == b, jnp.sum(hits[b], axis=1, keepdims=True), counts)
    counts = counts.astype(jnp.bfloat16)
    before = as_bf16(iota((ROWS, ROWS), 0) < iota((ROWS, ROWS), 1))
    source, other = iota((GROUP, GROUP), 0), iota((GROUP, GROUP), 1)
    start = jnp.sum(
        jnp.dot(counts, before, preferred_element_type=jnp.float32), axis=0, keepdims=True
    )
    off, pair_off = (
        (start + jnp.dot(as_bf16(other < limit), counts, preferred_element_type=jnp.float32)).astype(
            jnp.int32
        )
        for limit in (source, (source >> 1) * PAIR)
    )
    ranks = jnp.dot(
        jnp.concatenate(hits, axis=0).astype(jnp.bfloat16), before, preferred_element_type=jnp.float32
    )
    tile = pair_off >> 4
    inside = (off - tile * TILE).astype(jnp.float32)
    code = jnp.zeros((GROUP, ROWS), jnp.float32)
    for b in range(BINS):
        place = ranks[b * GROUP : (b + 1) * GROUP, :] + (inside[:, b : b + 1] + float(b * WINDOW))
        code = code + hits[b] * place
    return code.astype(jnp.int32), tile, start.astype(jnp.int32)


def windows(code_ref, pair):
    code = jnp.concatenate(
        [code_ref[pl.ds(pair * PAIR + i, 1), :] for i in range(PAIR)], axis=1
    )
    return as_bf16(iota((BINS * WINDOW, PAIR * ROWS), 0) == code)


def window_at(tile_ref, pair, b):
    return pl.ds(pl.multiple_of(tile_ref[pair * PAIR, b] * TILE, TILE), WINDOW)


def marks_of(id_row):
    marks = (iota((HEAD_DIM, ROWS), 0) == id_row).astype(jnp.float32)
    return jnp.transpose(marks)


def add_windows(tile_ref, code_ref, part_ref, id_ref, out_refs):
    for out_ref in out_refs:
        out_ref[...] = jnp.zeros_like(out_ref)

    def one_pair(pair, carry):
        moved = jnp.concatenate([part_ref[pair * PAIR + i, 0:ROWS, :] for i in range(PAIR)], axis=0)
        if len(out_refs) == 2:
            marks = jnp.concatenate(
                [marks_of(id_ref[pl.ds(pair * PAIR + i, 1), :]) for i in range(PAIR)], axis=0
            )
            moved = jnp.concatenate([moved, marks.astype(jnp.bfloat16)], axis=1)
        placed = jnp.dot(
            windows(code_ref, pair), moved, preferred_element_type=jnp.float32
        ).astype(jnp.bfloat16)
        for b in range(BINS):
            here = window_at(tile_ref, pair, b)
            for i, out_ref in enumerate(out_refs):
                block = placed[b * WINDOW : (b + 1) * WINDOW, i * HEAD_DIM : (i + 1) * HEAD_DIM]
                out_ref[here, :] = out_ref[here, :] + block
        return carry

    lax.fori_loop(0, GROUP // PAIR, one_pair, 0, unroll=2)


def key_kernel(part_ref, key_ref, mark_ref, id_ref, code_ref, tile_ref, start_ref, tiles, sem):
    ids = part_ref[:, ROWS : ROWS + EXTRA, :].astype(jnp.float32)[:, 0:1, :]
    ids = ids.reshape(GROUP, ROWS).astype(jnp.int32)
    code, tile, start = plan(ids)
    id_ref[...] = ids
    code_ref[...] = code
    tile_ref[...] = tile
    start_ref[...] = jnp.broadcast_to(start, start_ref.shape)
    copy = pltpu.make_async_copy(tile_ref, tiles, sem)
    copy.start()
    copy.wait()
    add_windows(tiles, code_ref, part_ref, id_ref, (key_ref, mark_ref))
    number = iota((8, HEAD_DIM), 1).astype(jnp.float32).astype(jnp.bfloat16)
    for chunk in range(GROUP):
        rows = slice(chunk * ROWS, (chunk + 1) * ROWS)
        samples = lax.dot_general(
            number, mark_ref[rows, :], (((1,), (1,)), ((), ())), preferred_element_type=jnp.float32
        )
        id_ref[chunk : chunk + 1, :] = samples[0:1, :].astype(jnp.int32)
    key_ref[PLACES : PLACES + GROUP, :] = id_ref[...].astype(jnp.float32).astype(jnp.bfloat16)
    id_ref[...] = ids
    marks = mark_ref[...].astype(jnp.float32)
    mark_ref[...] = (marks * MASKED - MASKED).astype(jnp.bfloat16)


def compact_key(part):
    table = jax.ShapeDtypeStruct((GROUP, ROWS), jnp.int32)
    rows = jax.ShapeDtypeStruct((LENGTH, HEAD_DIM), jnp.bfloat16)
    whole = pl.BlockSpec(memory_space=pltpu.VMEM)
    return pl.pallas_call(
        key_kernel,
        in_specs=[whole],
        out_specs=[whole] * 6,
        out_shape=[rows, rows, table, table, table, jax.ShapeDtypeStruct((8, ROWS), jnp.int32)],
        scratch_shapes=[pltpu.SMEM((GROUP, ROWS), jnp.int32), pltpu.SemaphoreType.DMA],
        compiler_params=pltpu.CompilerParams(vmem_limit_bytes=16 * 2**20),
        cost_estimate=pl.CostEstimate(
            flops=2 * PLACES * BINS * WINDOW * 2 * HEAD_DIM, bytes_accessed=3 * 2**20, transcendentals=0
        ),
        name="compact_key",
    )(part)


def mark_kernel(*refs):
    parts = len(refs) // 3
    for id_ref, mark_ref, start_ref in zip(refs[:parts], refs[parts::2], refs[parts + 1 :: 2]):
        ids = id_ref[...].astype(jnp.float32).astype(jnp.int32)
        bins = ids >> 1
        lane = iota((1, ROWS), 1)
        start = jnp.zeros((1, ROWS), jnp.float32)
        for b in range(1, BINS + 1):
            below = jnp.sum((bins < b).astype(jnp.float32), axis=1, keepdims=True)
            start = jnp.where(lane == b, jnp.sum(below, axis=0, keepdims=True), start)
        start_ref[...] = jnp.broadcast_to(start, start_ref.shape).astype(jnp.int32)
        for chunk in range(GROUP):
            marks = marks_of(ids[chunk : chunk + 1, :])
            mark_ref[chunk * ROWS : (chunk + 1) * ROWS, :] = (marks * MASKED - MASKED).astype(
                jnp.bfloat16
            )
        mark_ref[PLACES:, :] = jnp.full((LENGTH - PLACES, HEAD_DIM), -MASKED, jnp.bfloat16)


def remote_marks(parts):
    rows = jax.ShapeDtypeStruct((LENGTH, HEAD_DIM), jnp.bfloat16)
    start = jax.ShapeDtypeStruct((8, ROWS), jnp.int32)
    found = pl.pallas_call(
        mark_kernel,
        grid=(1,),
        in_specs=[pl.BlockSpec((GROUP, HEAD_DIM), lambda i: (PLACES // GROUP, 0))] * len(parts),
        out_specs=[
            pl.BlockSpec(shape, lambda i: (0, 0))
            for _ in parts
            for shape in ((LENGTH, HEAD_DIM), (8, ROWS))
        ],
        out_shape=[rows, start] * len(parts),
        compiler_params=pltpu.CompilerParams(vmem_limit_bytes=16 * 2**20),
        cost_estimate=pl.CostEstimate(flops=2**24, bytes_accessed=3 * 2**20, transcendentals=0),
        name="remote_marks",
    )(*parts)
    return found[::2], found[1::2]


def compact_kernel(kind, tile_ref, code_ref, id_ref, part_ref, *out_refs):
    add_windows(tile_ref, code_ref, part_ref, id_ref, out_refs)


def compact(kind, tables, part):
    ids, code, tile = tables
    length = QUERY_LENGTH if kind == "query" else LENGTH
    outs = 2 if kind == "query" else 1
    whole = pl.BlockSpec(memory_space=pltpu.VMEM)
    return pl.pallas_call(
        lambda *refs: compact_kernel(kind, *refs),
        in_specs=[pl.BlockSpec(memory_space=pltpu.SMEM), whole, whole, whole],
        out_specs=[whole] * outs,
        out_shape=[jax.ShapeDtypeStruct((length, HEAD_DIM), jnp.bfloat16)] * outs,
        compiler_params=pltpu.CompilerParams(vmem_limit_bytes=16 * 2**20),
        cost_estimate=pl.CostEstimate(
            flops=2 * PLACES * BINS * WINDOW * 2 * HEAD_DIM,
            bytes_accessed=2**20 + length * outs * HEAD_DIM * 2,
            transcendentals=0,
        ),
        name="compact_" + kind,
    )(tile, code, ids, part)


def attend_kernel(tile_ref, *refs):
    start_refs, (code_ref, query_ref, own_ref), refs = refs[:4], refs[4:7], refs[7:]
    key_refs, mark_refs, value_refs = refs[:4], refs[4:8], refs[8:12]
    out_ref, held_key, held_value, rows_ref = refs[12:]
    score_scale = 1.0 / math.sqrt(HEAD_DIM)
    nothing = jnp.concatenate(
        [
            jnp.zeros((KEY_TILE, HEAD_DIM), jnp.bfloat16),
            jnp.full((KEY_TILE, HEAD_DIM), -MASKED, jnp.bfloat16),
        ],
        axis=1,
    )
    held_key[...] = jnp.zeros_like(held_key)
    held_value[...] = jnp.zeros_like(held_value)
    rows_ref[...] = jnp.zeros_like(rows_ref)

    def attend_block(first, start, held, query_rows, key_rows):
        def clear(i, carry):
            held_key[pl.ds(pl.multiple_of(held + i * KEY_TILE, TILE), KEY_TILE), :] = nothing
            return carry

        lax.fori_loop(0, (key_rows - held + (KEY_TILE - 1)) >> 8, clear, 0)
        here = pl.ds(first, query_rows)
        query = jnp.concatenate([query_ref[here, :], own_ref[here, :]], axis=1)
        edges = list(range(0, key_rows, KEY_TILE)) + [key_rows]
        tiles = [slice(low, high) for low, high in zip(edges[:-1], edges[1:])]
        scores = [
            lax.dot_general(
                query, held_key[tile, :], (((1,), (1,)), ((), ())), preferred_element_type=jnp.float32
            )
            for tile in tiles
        ]
        row_max = jnp.max(scores[0], axis=1, keepdims=True)
        for part in scores[1:]:
            row_max = jnp.maximum(row_max, jnp.max(part, axis=1, keepdims=True))
        total = None
        for part, tile in zip(scores, tiles):
            weights = jnp.exp((part - row_max) * score_scale).astype(jnp.bfloat16)
            value = held_value[tile, :]
            wide = jnp.concatenate([value, jnp.ones_like(value)], axis=1)
            product = jnp.dot(weights, wide, preferred_element_type=jnp.float32)
            total = product if total is None else total + product
        result = (total[:, :HEAD_DIM] / total[:, HEAD_DIM:]).astype(jnp.bfloat16)
        own = iota((query_rows, HEAD_DIM), 0) >= start - first
        rows_ref[here, :] = jnp.where(own, result, rows_ref[here, :])

    def one_bin(b, carry):
        held = jnp.int32(0)
        for start_ref, *part_refs in zip(start_refs, key_refs, mark_refs, value_refs):
            first = (start_ref[0, b] >> 4) * TILE
            past = ((start_ref[0, b + 1] + (TILE - 1)) >> 4) * TILE

            def one_chunk(i, carry, first=first, held=held, part_refs=part_refs):
                key_ref, mark_ref, value_ref = part_refs
                source = pl.ds(pl.multiple_of(first + i * CHUNK, TILE), CHUNK)
                target = pl.ds(pl.multiple_of(held + i * CHUNK, TILE), CHUNK)
                held_key[target, :HEAD_DIM] = key_ref[source, :]
                held_key[target, HEAD_DIM:] = mark_ref[source, :]
                held_value[target, :] = value_ref[source, :]
                return carry

            lax.fori_loop(0, (past - first + (CHUNK - 1)) >> 7, one_chunk, 0)
            held = held + (past - first)
        start = start_refs[0][0, b]
        first = pl.multiple_of((start >> 4) * TILE, TILE)
        rows = ((start_refs[0][0, b + 1] + (TILE - 1)) >> 4) * TILE - first
        taken = jnp.bool_(False)
        for query_rows, key_rows in SIZES:
            fits = (rows <= query_rows) & (held <= key_rows)
            if (query_rows, key_rows) == SIZES[-1]:
                fits = jnp.bool_(True)

            @pl.when(fits & jnp.logical_not(taken))
            def _(query_rows=query_rows, key_rows=key_rows):
                attend_block(first, start, held, query_rows, key_rows)

            taken = taken | fits
        return carry

    lax.fori_loop(0, BINS, one_bin, 0)

    def one_pair(pair, carry):
        found = jnp.concatenate(
            [rows_ref[window_at(tile_ref, pair, b), :] for b in range(BINS)], axis=0
        )
        out_ref[pl.ds(pair * PAIR, PAIR)] = (
            lax.dot_general(
                windows(code_ref, pair),
                found,
                (((0,), (0,)), ((), ())),
                preferred_element_type=jnp.float32,
            )
            .astype(jnp.bfloat16)
            .reshape(PAIR, ROWS, HEAD_DIM)
        )
        return carry

    lax.fori_loop(0, GROUP // PAIR, one_pair, 0, unroll=2)


def attend(tables, starts, query, keys, marks, values):
    scalars = pl.BlockSpec(memory_space=pltpu.SMEM)
    whole = pl.BlockSpec(memory_space=pltpu.VMEM)
    pairs = BINS * 320 * 1152
    return pl.pallas_call(
        attend_kernel,
        in_specs=[scalars] * 5 + [whole] * 15,
        out_specs=whole,
        out_shape=jax.ShapeDtypeStruct((GROUP, ROWS, HEAD_DIM), jnp.bfloat16),
        scratch_shapes=[
            pltpu.VMEM((HELD, 2 * HEAD_DIM), jnp.bfloat16),
            pltpu.VMEM((HELD, HEAD_DIM), jnp.bfloat16),
            pltpu.VMEM((QUERY_LENGTH, HEAD_DIM), jnp.bfloat16),
        ],
        compiler_params=pltpu.CompilerParams(vmem_limit_bytes=26 * 2**20),
        cost_estimate=pl.CostEstimate(
            flops=8 * pairs * HEAD_DIM, bytes_accessed=16 * 2**20, transcendentals=pairs
        ),
        name="attend",
    )(tables[2], *starts, tables[1], *query, *keys, *marks, *values)


def finish_kernel(heads_ref, scale_ref, out_ref):
    for head in range(HEADS):
        columns = slice(head * HEAD_DIM, (head + 1) * HEAD_DIM)
        out_ref[:, columns] = (
            heads_ref[head].astype(jnp.float32) * (1.0 + scale_ref[:, columns])
        ).astype(jnp.bfloat16)


def finish(heads, row_scales):
    whole = pl.BlockSpec(memory_space=pltpu.VMEM)
    return pl.pallas_call(
        finish_kernel,
        in_specs=[whole, whole],
        out_specs=whole,
        out_shape=jax.ShapeDtypeStruct((ROWS, HEADS * HEAD_DIM), jnp.bfloat16),
        cost_estimate=pl.CostEstimate(flops=2**20, bytes_accessed=4 * 2**20, transcendentals=0),
        name="finish",
    )(heads, row_scales)


def shards(query_rows, key_rows, value_rows, seg_ids, timesteps, w_mod):
    raw_key = exchange(split_heads(key_rows, seg_ids[None, :]))
    split_value, split_query = lax.optimization_barrier(
        (split_heads(value_rows), split_heads(query_rows))
    )
    own_key, own_mark, *tables, own_start = compact_key(raw_key)
    chip_raw = from_chip(raw_key)
    own_value = compact("value", tables, exchange(split_value))[0]
    chip_raw, own_value = lax.optimization_barrier((chip_raw, own_value))
    chip_key, chip_mark, _, _, _, chip_start = compact_key(chip_raw)
    core_keys = [from_core(own_key), from_core(chip_key)]
    core_marks, core_starts = remote_marks(core_keys)
    query = compact("query", tables, exchange(split_query))
    chip_value, query, core_marks, core_starts = lax.optimization_barrier(
        (from_chip(own_value), query, core_marks, core_starts)
    )
    home = exchange(
        attend(
            tables,
            [own_start, chip_start, *core_starts],
            query,
            [own_key, chip_key, *core_keys],
            [own_mark, chip_mark, *core_marks],
            [own_value, chip_value, from_core(own_value), from_core(chip_value)],
        )
    )

    scale_table = scale_rows_table(timesteps, w_mod)
    lookup = (
        seg_ids[:, None] == jnp.arange(scale_table.shape[0], dtype=jnp.int32)[None, :]
    ).astype(jnp.float32)
    row_scales = jnp.dot(
        lookup, scale_table, precision=lax.Precision.HIGHEST, preferred_element_type=jnp.float32
    )
    return finish(home, row_scales)


def solution(mesh):
    placed = (
        P(("dp", "seq"), None),
        P(("dp", "seq"), None),
        P(("dp", "seq"), None),
        P(("dp", "seq")),
        P(),
        P(),
    )
    return jax.shard_map(
        shards, mesh=mesh, in_specs=placed, out_specs=P(("dp", "seq"), None), check_vma=False
    )
```

time: 236 us -> 168 us (0.71)
  Pallas kernels: 111 us -> 70.5 us
  local copies, waits for them, and re-layouts: 17.8 us -> 4.27 us
  waiting for transfers between devices: 62.1 us -> 50.3 us
    pallas_call x10 -> x6, Pallas kernels: 101 us -> 60 us  [the longest x1 29.9 us: attend(): pl.pallas_call(attend_kernel, in_specs=[scalars] * 5 + [whole] * 15, out_...]
    unnamed x30 -> x18, local copies, waits for them, and re-layouts: 17.2 us -> 4.27 us
    all_to_all x4, waiting for transfers between devices: 43.7 us -> 31.3 us  [exchange(): lax.all_to_all(blocks, AXES, 0, 0, tiled=True, axis_index_groups=head_gro...]
    ppermute x4, starting transfers between devices: 8.62 us -> 4.91 us  [from_core(): lax.ppermute(value, AXES, [(linear(x, y, z, c), linear(x, y, z, c ^ 1)) f...]
    ppermute x4, waiting for transfers between devices: 0.01 us -> 2.55 us  [from_core(): lax.ppermute(value, AXES, [(linear(x, y, z, c), linear(x, y, z, c ^ 1)) f...]
  transfers between devices with their start and end apart: 10 -> 10, of which waited for: 4 -> 5; matrix products, arithmetic and copies ran while one was open for 1% -> 2% of each run, Pallas kernels for 24% -> 21%
where the time goes in v2:
time: 168 us; the launch traced here: 167 us
  Pallas kernels  70.5 us (42%)
  waiting for transfers between devices  50.3 us (30%)
  starting transfers between devices  38.3 us (23%)
  local copies, waits for them, and re-layouts  4.27 us (3%)
  matrix products  2.79 us (2%)
    all_to_all x4, starting transfers between devices, exchange(): lax.all_to_all(blocks, AXES, 0, 0, tiled=True, axis_index_groups=head_gro...  33.3 us
    all_to_all x4, waiting for transfers between devices, exchange(): lax.all_to_all(blocks, AXES, 0, 0, tiled=True, axis_index_groups=head_gro...  31.3 us
    pallas_call x1, Pallas kernels, attend(): pl.pallas_call(attend_kernel, in_specs=[scalars] * 5 + [whole] * 15, out_...  29.9 us
    pallas_call x2, Pallas kernels, compact_key(): pl.pallas_call(key_kernel, in_specs=[whole], out_specs=[whole] * 6, out_s...  16.6 us
    ppermute x2, waiting for transfers between devices, from_chip(): lax.ppermute(value, AXES, [(linear(x, y, z, c), linear(x, y, z ^ 1, c)) f...  16.5 us
    pallas_call x2, Pallas kernels, compact(): pl.pallas_call(lambda *refs: compact_kernel(kind, *refs), in_specs=[pl.Bl...  11.7 us
    pallas_call x3, Pallas kernels, split_heads(): pl.pallas_call(split_kernel, in_specs=[whole] * len(operands), out_specs=...  7.33 us
    ppermute x4, starting transfers between devices, from_core(): lax.ppermute(value, AXES, [(linear(x, y, z, c), linear(x, y, z, c ^ 1)) f...  4.91 us
  transfers between devices with their start and end apart: 10, of which 5 were waited for; matrix products, arithmetic and copies ran while one was open for 2% of the time, Pallas kernels for 21%

profile of v2, /device:TPU:1, one launch (start us, length us, event | category | flops | bytes accessed | tf_op | source)
XLA Modules:
  0.0 166.5 jit_solution(18088615784513965565)
XLA Ops:
  0.0 2.6 %split_heads.3 = bf16[32,136,128]{2,1,0:T(8,128)(2,1)} custom-call(bf16[128,4096]{1,0:T(8,128)(2,1)} %rows_ref.3, s32[1,128]{1,0:T(1,128)} %bitcast.3), custom_call_target="tpu_custom_call" | custom-call | bytes 2097152 | tf_op jit(solution)/shard_map/split_heads/pallas_call | solution.py:90
  2.6 11.3 %all-to-all-start = ((bf16[32,136,128]{2,1,0:T(8,128)(2,1)}), bf16[32,136,128]{2,1,0:T(8,128)(2,1)S(1)}, u32[]{:S(2)}, u32[]{:S(2)}) async-start(bf16[32,136,128]{2,1,0:T(8,128)(2,1)} %split_heads.3), calls=%async_computation | async-start | bytes 2228224 | tf_op jit(solution)/shard_map/all_to_all | solution.py:37
  13.9 2.4 %split_heads.4 = bf16[32,128,128]{2,1,0:T(8,128)(2,1)} custom-call(bf16[128,4096]{1,0:T(8,128)(2,1)} %rows_ref.4), custom_call_target="tpu_custom_call" | custom-call | bytes 2097152 | tf_op jit(solution)/shard_map/split_heads/pallas_call | solution.py:90
  16.3 2.4 %split_heads.5 = bf16[32,128,128]{2,1,0:T(8,128)(2,1)} custom-call(bf16[128,4096]{1,0:T(8,128)(2,1)} %rows_ref.5), custom_call_target="tpu_custom_call" | custom-call | bytes 2097152 | tf_op jit(solution)/shard_map/split_heads/pallas_call | solution.py:90
  18.7 11.8 %all-to-all-done.part_ref = bf16[32,136,128]{2,1,0:T(8,128)(2,1)S(1)} async-done(((bf16[32,136,128]{2,1,0:T(8,128)(2,1)}), bf16[32,136,128]{2,1,0:T(8,128)(2,1)S(1)}, u32[]{:S(2)}, u32[]{:S(2)}) %all-to-all-start) | async-done | bytes 1114144 | tf_op jit(solution)/shard_map/all_to_all | solution.py:37
  30.5 6.2 %all-to-all-start.1 = ((bf16[32,128,128]{2,1,0:T(8,128)(2,1)}), bf16[32,128,128]{2,1,0:T(8,128)(2,1)}, u32[]{:S(2)}, u32[]{:S(2)}) async-start(bf16[32,128,128]{2,1,0:T(8,128)(2,1)} %split_heads.4), calls=%async_computation.1 | async-start | bytes 2097152 | tf_op jit(solution)/shard_map/all_to_all | solution.py:37
  36.7 0.1 collective-permute-start
  36.8 7.6 %compact_key.2 = (bf16[4224,128]{1,0:T(8,128)(2,1)}, bf16[4224,128]{1,0:T(8,128)(2,1)S(1)}, s32[32,128]{1,0:T(8,128)S(1)}, s32[32,128]{1,0:T(8,128)S(1)}, s32[32,128]{1,0:T(8,128)S(1)}, /*index=5*/s32[8,128]{1,0:T(8,128)S(1)}) custom-call(bf16[32,136,128]{2,1,0:T(8,128)(2,1)S(1)} %all-to-all-done.part_ref), custom_call_target="tpu_custom_call" | custom-call | flops 1610612736 | bytes 3145728 | tf_op jit(solution)/shard_map/compact_key/pallas_call | solution.py:220
  44.4 1.0 copy-done.2
  45.4 1.3 collective-permute-start.2
  46.7 5.5 %all-to-all-done.1.refs_3_ = bf16[32,128,128]{2,1,0:T(8,128)(2,1)} async-done(((bf16[32,128,128]{2,1,0:T(8,128)(2,1)}), bf16[32,128,128]{2,1,0:T(8,128)(2,1)}, u32[]{:S(2)}, u32[]{:S(2)}) %all-to-all-start.1) | async-done | bytes 1048608 | tf_op jit(solution)/shard_map/all_to_all | solution.py:37
  52.2 6.5 %all-to-all-start.2 = ((bf16[32,128,128]{2,1,0:T(8,128)(2,1)}), bf16[32,128,128]{2,1,0:T(8,128)(2,1)}, u32[]{:S(2)}, u32[]{:S(2)}) async-start(bf16[32,128,128]{2,1,0:T(8,128)(2,1)} %split_heads.5), calls=%async_computation.2 | async-start | bytes 2097152 | tf_op jit(solution)/shard_map/all_to_all | solution.py:37
  58.7 5.8 %compact_value.1.refs_15_ = bf16[4224,128]{1,0:T(8,128)(2,1)} custom-call(s32[32,128]{1,0:T(8,128)S(1)} %get-tuple-element.31.refs_0_.tile_ref, s32[32,128]{1,0:T(8,128)S(1)} %get-tuple-element.33.refs_1_.refs_4_, s32[32,128]{1,0:T(8,128)S(1)} %get-tuple-element.34.refs_2_, bf16[32,128,128]{2,1,0:T(8,128)(2,1)} %all-to-all-done.1.refs_3_), custom_call_target="tpu_custom_call" | custom-call | flops 1610612736 | bytes 2129920 | tf_op jit(solution)/shard_map/compact_value/pallas_call | solution.py:282
  64.6 8.9 %compact_key.3 = (bf16[4224,128]{1,0:T(8,128)(2,1)}, bf16[4224,128]{1,0:T(8,128)(2,1)S(1)}, s32[32,128]{1,0:T(8,128)}, s32[32,128]{1,0:T(8,128)}, s32[32,128]{1,0:T(8,128)}, /*index=5*/s32[8,128]{1,0:T(8,128)S(1)}) custom-call(bf16[32,136,128]{2,1,0:T(8,128)(2,1)} %collective-permute-done.part_ref), custom_call_target="tpu_custom_call" | custom-call | flops 1610612736 | bytes 3145728 | tf_op jit(solution)/shard_map/compact_key/pallas_call | solution.py:220
  73.5 1.1 copy-done.4
  74.6 1.3 collective-permute-start.3
  75.9 5.9 %compact_query.1 = (bf16[4624,128]{1,0:T(8,128)(2,1)S(1)}, bf16[4624,128]{1,0:T(8,128)(2,1)S(1)}) custom-call(s32[32,128]{1,0:T(8,128)S(1)} %get-tuple-element.31.refs_0_.tile_ref, s32[32,128]{1,0:T(8,128)S(1)} %get-tuple-element.33.refs_1_.refs_4_, s32[32,128]{1,0:T(8,128)S(1)} %get-tuple-element.34.refs_2_, bf16[32,128,128]{2,1,0:T(8,128)(2,1)} %all-to-all-done.2.refs_3_), custom_call_target="tpu_custom_call" | custom-call | flops 1610612736 | bytes 3416064 | tf_op jit(solution)/shard_map/compact_query/pallas_call | solution.py:282
  81.8 1.6 collective-permute-start.4
  83.4 1.8 %remote_marks.1 = (bf16[4224,128]{1,0:T(8,128)(2,1)S(1)}, s32[8,128]{1,0:T(8,128)S(1)}, bf16[4224,128]{1,0:T(8,128)(2,1)S(1)}, s32[8,128]{1,0:T(8,128)S(1)}) custom-call(bf16[4224,128]{1,0:T(8,128)(2,1)} %collective-permute-done.2.refs_0_.refs_9_, bf16[4224,128]{1,0:T(8,128)(2,1)S(1)} %collective-permute-done.3.refs_1_.refs_10_), custom_call_target="tpu_custom_call" | custom-call | flops 16777216 | bytes 3145728 | tf_op jit(solution)/shard_map/remote_marks/pallas_call | solution.py:256
  85.2 16.5 %collective-permute-done.1.refs_16_ = bf16[4224,128]{1,0:T(8,128)(2,1)} collective-permute-done((bf16[4224,128]{1,0:T(8,128)(2,1)}, bf16[4224,128]{1,0:T(8,128)(2,1)}, u32[]{:S(2)}, u32[]{:S(2)}) %collective-permute-start.1) | collective-permute-done | bytes 1081376 | tf_op jit(solution)/shard_map/ppermute | solution.py:53
  101.7 0.8 collective-permute-start.5
  102.4 2.5 %collective-permute-done.5.refs_18_ = bf16[4224,128]{1,0:T(8,128)(2,1)S(1)} collective-permute-done((bf16[4224,128]{1,0:T(8,128)(2,1)}, bf16[4224,128]{1,0:T(8,128)(2,1)S(1)}, u32[]{:S(2)}, u32[]{:S(2)}) %collective-permute-start.5) | collective-permute-done | bytes 1081376 | tf_op jit(solution)/shard_map/ppermute | solution.py:59
  105.0 29.9 %attend.1 = bf16[32,128,128]{2,1,0:T(8,128)(2,1)S(1)} custom-call(s32[32,128]{1,0:T(8,128)S(1)} %get-tuple-element.31.refs_0_.tile_ref, s32[8,128]{1,0:T(8,128)S(1)} %get-tuple-element.32.refs_0_, s32[8,128]{1,0:T(8,128)S(1)} %get-tuple-element.37.refs_1_, s32[8,128]{1,0:T(8,128)S(1)} %get-tuple-element.48.refs_2_, s32[8,128]{1,0:T(8,128)S(1)} %get-tuple-element.49.refs_3_, ...), custom_call_target="tpu_custom_call" | custom-call | flops 6039797760 | bytes 16777216 | tf_op jit(solution)/shard_map/attend/pallas_call | solution.py:401
  134.9 1.0 copy-done.1
  135.9 9.3 %all-to-all-start.3 = ((bf16[32,128,128]{2,1,0:T(8,128)(2,1)}), bf16[32,128,128]{2,1,0:T(8,128)(2,1)S(1)}, u32[]{:S(2)}, u32[]{:S(2)}) async-start(bf16[32,128,128]{2,1,0:T(8,128)(2,1)} %copy-done.1), calls=%async_computation.3 | async-start | bytes 2097152 | tf_op jit(solution)/shard_map/all_to_all | solution.py:37
  145.2 0.1 multiply_cosine_fusion
  145.4 0.4 fusion.2
  145.8 0.2 copy-done.7
  146.0 2.4 %fusion.scale_ref = f32[128,4096]{1,0:T(8,128)} fusion(f32[32,4096]{1,0:T(8,128)S(1)} %fusion.2, s32[128]{0:T(128)S(1)} %copy-done.7), kind=kOutput, calls=%fused_computation.1 | convolution fusion | flops 201330688 | bytes 2621952 | tf_op jit(solution)/shard_map/dot_general | solution.py:470
  148.4 14.0 %all-to-all-done.3.heads_ref = bf16[32,128,128]{2,1,0:T(8,128)(2,1)S(1)} async-done(((bf16[32,128,128]{2,1,0:T(8,128)(2,1)}), bf16[32,128,128]{2,1,0:T(8,128)(2,1)S(1)}, u32[]{:S(2)}, u32[]{:S(2)}) %all-to-all-start.3) | async-done | bytes 1048608 | tf_op jit(solution)/shard_map/all_to_all | solution.py:37
  162.3 1.0 copy-done.6
  163.3 3.2 %finish.1 = bf16[128,4096]{1,0:T(8,128)(2,1)} custom-call(bf16[32,128,128]{2,1,0:T(8,128)(2,1)} %copy-done.6, f32[128,4096]{1,0:T(8,128)} %fusion.scale_ref), custom_call_target="tpu_custom_call" | custom-call | flops 1048576 | bytes 4194304 | tf_op jit(solution)/shard_map/finish/pallas_call | solution.py:429
  (21 shorter events, 0.1 us)
Async XLA Ops:
  0.0 145.3 %copy-start = (bf16[256,4096]{1,0:T(8,128)(2,1)S(1)}, bf16[256,4096]{1,0:T(8,128)(2,1)}, u32[]{:S(2)}) copy-start(bf16[256,4096]{1,0:T(8,128)(2,1)} %param.11) | copy-start | bytes 6291460
  2.6 27.9 %all-to-all-start = ((bf16[32,136,128]{2,1,0:T(8,128)(2,1)}), bf16[32,136,128]{2,1,0:T(8,128)(2,1)S(1)}, u32[]{:S(2)}, u32[]{:S(2)}) async-start(bf16[32,136,128]{2,1,0:T(8,128)(2,1)} %split_heads.3), calls=%async_computation | async-start | bytes 2228224 | tf_op jit(solution)/shard_map/all_to_all | solution.py:37
  30.5 21.7 %all-to-all-start.1 = ((bf16[32,128,128]{2,1,0:T(8,128)(2,1)}), bf16[32,128,128]{2,1,0:T(8,128)(2,1)}, u32[]{:S(2)}, u32[]{:S(2)}) async-start(bf16[32,128,128]{2,1,0:T(8,128)(2,1)} %split_heads.4), calls=%async_computation.1 | async-start | bytes 2097152 | tf_op jit(solution)/shard_map/all_to_all | solution.py:37
  36.7 27.9 %collective-permute-start = (bf16[32,136,128]{2,1,0:T(8,128)(2,1)S(1)}, bf16[32,136,128]{2,1,0:T(8,128)(2,1)}, u32[]{:S(2)}, u32[]{:S(2)}) collective-permute-start(bf16[32,136,128]{2,1,0:T(8,128)(2,1)S(1)} %all-to-all-done.part_ref), channel_id=1, source_target_pairs={{0,8},{1,9},{8,0},{9,1},{16,24},{17,25},{24,16},{25,17},{2,10},{3,... | collective-permute-start | bytes 3342344 | tf_op jit(solution)/shard_map/ppermute | solution.py:53
  44.4 1.0 copy-start.2
  45.4 37.9 %collective-permute-start.2 = (bf16[4224,128]{1,0:T(8,128)(2,1)}, bf16[4224,128]{1,0:T(8,128)(2,1)}, u32[]{:S(2)}, u32[]{:S(2)}) collective-permute-start(bf16[4224,128]{1,0:T(8,128)(2,1)} %get-tuple-element.42.refs_7_), channel_id=1, source_target_pairs={{0,1},{1,0},{8,9},{9,8},{16,17},{17,16},{24,25},{25,24},{2,3},{3,2... | collective-permute-start | bytes 3244040 | tf_op jit(solution)/shard_map/ppermute | solution.py:59
  52.2 23.6 %all-to-all-start.2 = ((bf16[32,128,128]{2,1,0:T(8,128)(2,1)}), bf16[32,128,128]{2,1,0:T(8,128)(2,1)}, u32[]{:S(2)}, u32[]{:S(2)}) async-start(bf16[32,128,128]{2,1,0:T(8,128)(2,1)} %split_heads.5), calls=%async_computation.2 | async-start | bytes 2097152 | tf_op jit(solution)/shard_map/all_to_all | solution.py:37
  73.5 1.1 copy-start.4
  74.6 8.8 %collective-permute-start.3 = (bf16[4224,128]{1,0:T(8,128)(2,1)}, bf16[4224,128]{1,0:T(8,128)(2,1)S(1)}, u32[]{:S(2)}, u32[]{:S(2)}) collective-permute-start(bf16[4224,128]{1,0:T(8,128)(2,1)} %get-tuple-element.43.refs_8_), channel_id=1, source_target_pairs={{0,1},{1,0},{8,9},{9,8},{16,17},{17,16},{24,25},{25,24},{2,3},{3,2... | collective-permute-start | bytes 3244040 | tf_op jit(solution)/shard_map/ppermute | solution.py:59
  75.8 25.8 %collective-permute-start.1 = (bf16[4224,128]{1,0:T(8,128)(2,1)}, bf16[4224,128]{1,0:T(8,128)(2,1)}, u32[]{:S(2)}, u32[]{:S(2)}) collective-permute-start(bf16[4224,128]{1,0:T(8,128)(2,1)} %compact_value.1.refs_15_), channel_id=1, source_target_pairs={{0,8},{1,9},{8,0},{9,1},{16,24},{17,25},{24,16},{25,17},{2,10},{3,... | collective-permute-start | bytes 3244040 | tf_op jit(solution)/shard_map/ppermute | solution.py:53
  81.8 23.2 %copy-start.3 = (bf16[4224,128]{1,0:T(8,128)(2,1)S(1)}, bf16[4224,128]{1,0:T(8,128)(2,1)}, u32[]{:S(2)}) copy-start(bf16[4224,128]{1,0:T(8,128)(2,1)} %copy-done.2) | copy-start | bytes 3244036
  81.8 23.2 %copy-start.5 = (bf16[4224,128]{1,0:T(8,128)(2,1)S(1)}, bf16[4224,128]{1,0:T(8,128)(2,1)}, u32[]{:S(2)}) copy-start(bf16[4224,128]{1,0:T(8,128)(2,1)} %copy-done.4) | copy-start | bytes 3244036
  81.8 20.7 %collective-permute-start.4 = (bf16[4224,128]{1,0:T(8,128)(2,1)}, bf16[4224,128]{1,0:T(8,128)(2,1)S(1)}, u32[]{:S(2)}, u32[]{:S(2)}) collective-permute-start(bf16[4224,128]{1,0:T(8,128)(2,1)} %compact_value.1.refs_15_), channel_id=1, source_target_pairs={{0,1},{1,0},{8,9},{9,8},{16,17},{17,16},{24,25},{25,24},{2,3},{3,2... | collective-permute-start | bytes 3244040 | tf_op jit(solution)/shard_map/ppermute | solution.py:59
  101.7 3.3 %collective-permute-start.5 = (bf16[4224,128]{1,0:T(8,128)(2,1)}, bf16[4224,128]{1,0:T(8,128)(2,1)S(1)}, u32[]{:S(2)}, u32[]{:S(2)}) collective-permute-start(bf16[4224,128]{1,0:T(8,128)(2,1)} %collective-permute-done.1.refs_16_), channel_id=1, source_target_pairs={{0,1},{1,0},{8,9},{9,8},{16,17},{17,16},{24,25},{25,24},{2,3},{3,2... | collective-permute-start | bytes 3244040 | tf_op jit(solution)/shard_map/ppermute | solution.py:59
  134.9 1.0 copy-start.1
  135.9 9.3 %copy-start.8 = (s32[32]{0:T(128)S(1)}, s32[32]{0:T(128)}, u32[]{:S(2)}) copy-start(s32[32]{0:T(128)} %param.10) | copy-start | bytes 388
  135.9 26.5 %all-to-all-start.3 = ((bf16[32,128,128]{2,1,0:T(8,128)(2,1)}), bf16[32,128,128]{2,1,0:T(8,128)(2,1)S(1)}, u32[]{:S(2)}, u32[]{:S(2)}) async-start(bf16[32,128,128]{2,1,0:T(8,128)(2,1)} %copy-done.1), calls=%async_computation.3 | async-start | bytes 2097152 | tf_op jit(solution)/shard_map/all_to_all | solution.py:37
  145.3 0.7 copy-start.7
  162.3 1.0 copy-start.6
